TPU v7x, 32 devices: a whole 2x2x4 slice. The times are simulated.
32 devices in a mesh: dp: 16 (over z, y, core), tensor: 2 (over x).
Axes of the slice: x: 2, y: 2, z: 4, core: 2. Of those that a mesh axis runs over, the one named last changes fastest.
Arguments:
- tokens: bfloat16 [32, 448, 1024], P('dp'), may hold values from -6 to 6
- encoded: bfloat16 [32, 1500, 1024], P('dp'), may hold values from -6 to 6
- cotangent: bfloat16 [32, 448, 1024], P('dp'), may hold values from -6 to 6
- self_gain: bfloat16 [1024], replicated, may hold values from 0.5 to 1.5
- self_shift: bfloat16 [1024], replicated, may hold values from -1.75 to 1.75
- self_query: bfloat16 [1024, 1024], P(None, 'tensor'), may hold values from -0.25 to 0.25
- self_query_bias: bfloat16 [1024], P('tensor'), may hold values from -1.75 to 1.75
- self_key: bfloat16 [1024, 1024], P(None, 'tensor'), may hold values from -0.1875 to 0.1875
- self_value: bfloat16 [1024, 1024], P(None, 'tensor'), may hold values from -0.1875 to 0.1875
- self_value_bias: bfloat16 [1024], P('tensor'), may hold values from -1.75 to 1.75
- self_mixer: bfloat16 [1024, 1024], P('tensor'), may hold values from -0.5 to 0.5
- self_mixer_bias: bfloat16 [1024], replicated, may hold values from -1.75 to 1.75
- cross_gain: bfloat16 [1024], replicated, may hold values from 0.5 to 1.5
- cross_shift: bfloat16 [1024], replicated, may hold values from -1.75 to 1.75
- cross_query: bfloat16 [1024, 1024], P(None, 'tensor'), may hold values from -0.25 to 0.25
- cross_query_bias: bfloat16 [1024], P('tensor'), may hold values from -1.75 to 1.75
- cross_key: bfloat16 [1024, 1024], P(None, 'tensor'), may hold values from -0.1875 to 0.1875
- cross_value: bfloat16 [1024, 1024], P(None, 'tensor'), may hold values from -0.1875 to 0.1875
- cross_value_bias: bfloat16 [1024], P('tensor'), may hold values from -1.75 to 1.75
- cross_mixer: bfloat16 [1024, 1024], P('tensor'), may hold values from -0.75 to 0.75
- cross_mixer_bias: bfloat16 [1024], replicated, may hold values from -1.75 to 1.75
- feed_gain: bfloat16 [1024], replicated, may hold values from 0.5 to 1.5
- feed_shift: bfloat16 [1024], replicated, may hold values from -1.75 to 1.75
- expand_weight: bfloat16 [1024, 4096], P(None, 'tensor'), may hold values from -0.1875 to 0.1875
- expand_bias: bfloat16 [4096], P('tensor'), may hold values from -3 to 3
- reduce_weight: bfloat16 [4096, 1024], P('tensor'), may hold values from -0.125 to 0.125
- reduce_bias: bfloat16 [1024], replicated, may hold values from -1.75 to 1.75
Outputs:
- output: float32 [32, 448, 1024], P('dp')
- grad_tokens: float32 [32, 448, 1024], P('dp')
- grad_encoded: float32 [32, 1500, 1024], P('dp', None, 'tensor')
- grad_self_gain: float32 [1024], replicated
- grad_self_shift: float32 [1024], replicated
- grad_self_query: float32 [1024, 1024], P(None, 'tensor')
- grad_self_query_bias: float32 [1024], P('tensor')
- grad_self_key: float32 [1024, 1024], P(None, 'tensor')
- grad_self_value: float32 [1024, 1024], P(None, 'tensor')
- grad_self_value_bias: float32 [1024], P('tensor')
- grad_self_mixer: float32 [1024, 1024], P('tensor')
- grad_self_mixer_bias: float32 [1024], replicated
- grad_cross_gain: float32 [1024], replicated
- grad_cross_shift: float32 [1024], replicated
- grad_cross_query: float32 [1024, 1024], P(None, 'tensor')
- grad_cross_query_bias: float32 [1024], P('tensor')
- grad_cross_key: float32 [1024, 1024], P(None, 'tensor')
- grad_cross_value: float32 [1024, 1024], P(None, 'tensor')
- grad_cross_value_bias: float32 [1024], P('tensor')
- grad_cross_mixer: float32 [1024, 1024], P('tensor')
- grad_cross_mixer_bias: float32 [1024], replicated
- grad_feed_gain: float32 [1024], replicated
- grad_feed_shift: float32 [1024], replicated
- grad_expand_weight: float32 [1024, 4096], P(None, 'tensor')
- grad_expand_bias: float32 [4096], P('tensor')
- grad_reduce_weight: float32 [4096, 1024], P('tensor')
- grad_reduce_bias: float32 [1024], replicated
All inputs are finite; a program needn't handle non-finite values.
Results may differ from a plain program's by a relative error of at most 0.022.
Values may be sent and summed in bfloat16 or wider, within the bound.
No kernel may reach another device: no remote copies, remote signals or barrier semaphores. Data moves between devices by JAX's collectives and lax.ppermute only.
A program may use at most 256 MiB of HBM per device.

v0:
```python
import math
import jax
import jax.numpy as jnp
from jax import lax
from jax.sharding import PartitionSpec as P

HEAD = 64
EPSILON = 1e-05
F32 = jnp.float32
BF16 = jnp.bfloat16


def normalize(values, norm_gain, norm_shift):
    row_mean = jnp.mean(values, axis=-1, keepdims=True)
    centered = values - row_mean
    spread = jnp.mean(centered * centered, axis=-1, keepdims=True)
    inverse = lax.rsqrt(spread + EPSILON)
    normed = centered * inverse
    return (normed * norm_gain + norm_shift, normed, inverse)


def normalize_back(grad_out, normed, inverse, norm_gain):
    scaled = grad_out * norm_gain
    centre = jnp.mean(scaled, axis=-1, keepdims=True)
    row_along = jnp.mean(scaled * normed, axis=-1, keepdims=True)
    grad_in = inverse * (scaled - centre - normed * row_along)
    return (grad_in, jnp.sum(grad_out * normed, axis=0), jnp.sum(grad_out, axis=0))


def scores_of(queries, key_heads, causal):
    scaling = 1.0 / math.sqrt(queries.shape[-1])
    scores = jnp.einsum("lhe,khe->hlk", queries, key_heads, preferred_element_type=F32) * scaling
    if causal:
        row_index = lax.broadcasted_iota(jnp.int32, scores.shape[-2:], 0)
        col_index = lax.broadcasted_iota(jnp.int32, scores.shape[-2:], 1)
        scores = jnp.where(col_index <= row_index, scores, -1e30)
    return scores


def attend(queries, key_heads, value_heads, causal):
    scores = scores_of(queries, key_heads, causal)
    highest = jnp.max(scores, axis=-1, keepdims=True)
    denominator = jnp.sum(jnp.exp(scores - highest), axis=-1, keepdims=True)
    logsum = highest + jnp.log(denominator)
    probs = jnp.exp(scores - logsum)
    mixture = jnp.einsum(
        "hlk,khe->lhe", probs.astype(BF16), value_heads, preferred_element_type=F32
    )
    return (mixture.astype(BF16), logsum)


def attend_back(grad_mixture, queries, key_heads, value_heads, logsum, causal):
    scaling = 1.0 / math.sqrt(queries.shape[-1])
    probs = jnp.exp(scores_of(queries, key_heads, causal) - logsum)
    grad_probs = jnp.einsum("lhe,khe->hlk", grad_mixture, value_heads, preferred_element_type=F32)
    row_dot = jnp.sum(grad_probs * probs, axis=-1, keepdims=True)
    grad_scores = (probs * (grad_probs - row_dot)).astype(BF16)
    grad_queries = (
        jnp.einsum("hlk,khe->lhe", grad_scores, key_heads, preferred_element_type=F32) * scaling
    ).astype(BF16)
    grad_keys = (
        jnp.einsum("hlk,lhe->khe", grad_scores, queries, preferred_element_type=F32) * scaling
    ).astype(BF16)
    grad_values = jnp.einsum(
        "hlk,lhe->khe", probs.astype(BF16), grad_mixture, preferred_element_type=F32
    ).astype(BF16)
    return (grad_queries, grad_keys, grad_values)


def project(inputs, weight):
    return jnp.dot(inputs, weight, preferred_element_type=F32)


def project_back(grads, weight):
    return jnp.einsum("lc,dc->ld", grads, weight, preferred_element_type=F32)


def weight_grad(inputs, grads):
    left = jnp.concatenate(inputs, axis=0)
    right = jnp.concatenate(grads, axis=0)
    return jnp.einsum("ld,lc->dc", left, right, preferred_element_type=F32).astype(BF16)


def column_sum(grads):
    return jnp.sum(grads.astype(F32), axis=0)


def tensor_sum(partial):
    if lax.axis_size("tensor") != 2:
        return lax.psum(partial, "tensor")
    mine = lax.optimization_barrier(partial.astype(BF16))
    other = lax.ppermute(mine, "tensor", [(0, 1), (1, 0)])
    return mine.astype(F32) + other.astype(F32)


def dp_sum(grads):
    share = lax.psum_scatter(grads, "dp", scatter_dimension=0, tiled=True)
    return lax.all_gather(share, "dp", axis=0, tiled=True)


def local(
    tokens,
    encoded,
    cotangent,
    self_gain,
    self_shift,
    self_query,
    self_query_bias,
    self_key,
    self_value,
    self_value_bias,
    self_mixer,
    self_mixer_bias,
    cross_gain,
    cross_shift,
    cross_query,
    cross_query_bias,
    cross_key,
    cross_value,
    cross_value_bias,
    cross_mixer,
    cross_mixer_bias,
    feed_gain,
    feed_shift,
    expand_weight,
    expand_bias,
    reduce_weight,
    reduce_bias,
):
    clips, length, width = tokens.shape
    frames = encoded.shape[1]
    local_width = self_query.shape[1]
    head_count = local_width // HEAD
    gain_one = self_gain.astype(F32)
    gain_two = cross_gain.astype(F32)
    gain_three = feed_gain.astype(F32)
    each = range(clips)

    def heads(values):
        return values.reshape(values.shape[0], head_count, HEAD)

    def flat(values):
        return values.reshape(values.shape[0], local_width)

    source, normed_one, inverse_one, attn_in = ([], [], [], [])
    self_queries, self_keys, self_values = ([], [], [])
    self_mixture, self_logsum, self_sum = ([], [], [])
    cross_keys, cross_values = ([], [])
    for i in each:
        source.append(tokens[i].astype(F32))
        normed, plain, inverse = normalize(source[i], gain_one, self_shift.astype(F32))
        normed_one.append(plain)
        inverse_one.append(inverse)
        attn_in.append(normed.astype(BF16))
        self_queries.append(
            (project(attn_in[i], self_query) + self_query_bias.astype(F32)).astype(BF16)
        )
        self_keys.append(project(attn_in[i], self_key).astype(BF16))
        self_values.append(
            (project(attn_in[i], self_value) + self_value_bias.astype(F32)).astype(BF16)
        )
        mixed, logsum = attend(
            heads(self_queries[i]), heads(self_keys[i]), heads(self_values[i]), True
        )
        self_mixture.append(flat(mixed))
        self_logsum.append(logsum)
        self_sum.append(tensor_sum(project(self_mixture[i], self_mixer)))
    for i in each:
        cross_keys.append(project(encoded[i], cross_key).astype(BF16))
        cross_values.append(
            (project(encoded[i], cross_value) + cross_value_bias.astype(F32)).astype(BF16)
        )
    hidden_one, normed_two, inverse_two, cross_in = ([], [], [], [])
    cross_queries, cross_mixture, cross_logsum, cross_sum = ([], [], [], [])
    for i in each:
        hidden_one.append(source[i] + self_sum[i] + self_mixer_bias.astype(F32))
        normed, plain, inverse = normalize(hidden_one[i], gain_two, cross_shift.astype(F32))
        normed_two.append(plain)
        inverse_two.append(inverse)
        cross_in.append(normed.astype(BF16))
        cross_queries.append(
            (project(cross_in[i], cross_query) + cross_query_bias.astype(F32)).astype(BF16)
        )
        mixed, logsum = attend(
            heads(cross_queries[i]), heads(cross_keys[i]), heads(cross_values[i]), False
        )
        cross_mixture.append(flat(mixed))
        cross_logsum.append(logsum)
        cross_sum.append(tensor_sum(project(cross_mixture[i], cross_mixer)))
    hidden_two, normed_three, inverse_three, feed_in = ([], [], [], [])
    activated, grad_preact, feed_grad, feed_sum = ([], [], [], [])
    for i in each:
        hidden_two.append(hidden_one[i] + cross_sum[i] + cross_mixer_bias.astype(F32))
        normed, plain, inverse = normalize(hidden_two[i], gain_three, feed_shift.astype(F32))
        normed_three.append(plain)
        inverse_three.append(inverse)
        feed_in.append(normed.astype(BF16))
        preact = project(feed_in[i], expand_weight) + expand_bias.astype(F32)
        grad_activated = project_back(cotangent[i], reduce_weight)
        cdf = 0.5 * (1.0 + lax.erf(preact * (1.0 / math.sqrt(2.0))))
        density = jnp.exp(-0.5 * preact * preact) * (1.0 / math.sqrt(2.0 * math.pi))
        activated.append((preact * cdf).astype(BF16))
        grad_preact.append((grad_activated * (cdf + preact * density)).astype(BF16))
        feed_grad.append(tensor_sum(project_back(grad_preact[i], expand_weight)))
    for i in each:
        feed_sum.append(tensor_sum(project(activated[i], reduce_weight)))
    output = [hidden_two[i] + feed_sum[i] + reduce_bias.astype(F32) for i in each]
    grad_out = [cotangent[i].astype(F32) for i in each]
    grad_reduce_weight = dp_sum(weight_grad(activated, [cotangent[i] for i in each]))
    grad_expand_weight = dp_sum(weight_grad(feed_in, grad_preact))
    grad_reduce_bias = sum((jnp.sum(grad_out[i], axis=0) for i in each))
    grad_expand_bias = sum((column_sum(grad_preact[i]) for i in each))
    grad_two, two_rounded, feed_gains, feed_shifts = ([], [], [], [])
    cross_query_grad, cross_key_grad, cross_value_grad = ([], [], [])
    cross_grad = []
    for i in each:
        norm_grad, part_gain, part_shift = normalize_back(
            feed_grad[i], normed_three[i], inverse_three[i], gain_three
        )
        feed_gains.append(part_gain)
        feed_shifts.append(part_shift)
        grad_two.append(grad_out[i] + norm_grad)
        two_rounded.append(grad_two[i].astype(BF16))
        grad_cross_mixture = project_back(two_rounded[i], cross_mixer).astype(BF16)
        query_grad, key_grad, value_grad = attend_back(
            heads(grad_cross_mixture),
            heads(cross_queries[i]),
            heads(cross_keys[i]),
            heads(cross_values[i]),
            cross_logsum[i],
            False,
        )
        cross_query_grad.append(flat(query_grad))
        cross_key_grad.append(flat(key_grad))
        cross_value_grad.append(flat(value_grad))
        cross_grad.append(tensor_sum(project_back(cross_query_grad[i], cross_query)))
    grad_cross_mixer = dp_sum(weight_grad(cross_mixture, two_rounded))
    grad_cross_query = dp_sum(weight_grad(cross_in, cross_query_grad))
    frames_in = [encoded[i] for i in each]
    grad_cross_key = dp_sum(weight_grad(frames_in, cross_key_grad))
    grad_cross_value = dp_sum(weight_grad(frames_in, cross_value_grad))
    part_cross_mixer_bias = sum((jnp.sum(grad_two[i], axis=0) for i in each))
    grad_cross_query_bias = sum((column_sum(cross_query_grad[i]) for i in each))
    grad_cross_value_bias = sum((column_sum(cross_value_grad[i]) for i in each))
    grad_one, one_rounded, cross_gains, cross_shifts = ([], [], [], [])
    query_grads, key_grads, value_grads, self_grad = ([], [], [], [])
    for i in each:
        norm_grad, part_gain, part_shift = normalize_back(
            cross_grad[i], normed_two[i], inverse_two[i], gain_two
        )
        cross_gains.append(part_gain)
        cross_shifts.append(part_shift)
        grad_one.append(grad_two[i] + norm_grad)
        one_rounded.append(grad_one[i].astype(BF16))
        grad_self_mixture = project_back(one_rounded[i], self_mixer).astype(BF16)
        query_grad, key_grad, value_grad = attend_back(
            heads(grad_self_mixture),
            heads(self_queries[i]),
            heads(self_keys[i]),
            heads(self_values[i]),
            self_logsum[i],
            True,
        )
        query_grads.append(flat(query_grad))
        key_grads.append(flat(key_grad))
        value_grads.append(flat(value_grad))
        self_terms = (
            project_back(query_grads[i], self_query)
            + project_back(key_grads[i], self_key)
            + project_back(value_grads[i], self_value)
        )
        self_grad.append(tensor_sum(self_terms))
    grad_self_mixer = dp_sum(weight_grad(self_mixture, one_rounded))
    grad_self_query = dp_sum(weight_grad(attn_in, query_grads))
    grad_self_key = dp_sum(weight_grad(attn_in, key_grads))
    grad_self_value = dp_sum(weight_grad(attn_in, value_grads))
    part_self_mixer_bias = sum((jnp.sum(grad_one[i], axis=0) for i in each))
    grad_self_query_bias = sum((column_sum(query_grads[i]) for i in each))
    grad_self_value_bias = sum((column_sum(value_grads[i]) for i in each))
    grad_encoded = []
    members = lax.axis_size("tensor")
    share = width // members
    for i in each:
        if members == 2:
            me = lax.axis_index("tensor")

            def terms(part):
                rows_key = lax.dynamic_slice_in_dim(cross_key, part * share, share, 0)
                rows_value = lax.dynamic_slice_in_dim(cross_value, part * share, share, 0)
                return project_back(cross_key_grad[i], rows_key) + project_back(
                    cross_value_grad[i], rows_value
                )

            other = lax.ppermute(terms(1 - me).astype(BF16), "tensor", [(0, 1), (1, 0)])
            grad_encoded.append(terms(me) + other.astype(F32))
        else:
            frame_terms = project_back(cross_key_grad[i], cross_key) + project_back(
                cross_value_grad[i], cross_value
            )
            grad_encoded.append(
                lax.psum_scatter(frame_terms, "tensor", scatter_dimension=1, tiled=True)
            )
    self_gains, self_shifts, grad_tokens = ([], [], [])
    for i in each:
        norm_grad, part_gain, part_shift = normalize_back(
            self_grad[i], normed_one[i], inverse_one[i], gain_one
        )
        self_gains.append(part_gain)
        self_shifts.append(part_shift)
        grad_tokens.append(grad_one[i] + norm_grad)
    vectors = [
        sum(self_gains),
        sum(self_shifts),
        part_self_mixer_bias,
        sum(cross_gains),
        sum(cross_shifts),
        part_cross_mixer_bias,
        sum(feed_gains),
        sum(feed_shifts),
        grad_reduce_bias,
        grad_self_query_bias,
        grad_self_value_bias,
        grad_cross_query_bias,
        grad_cross_value_bias,
        grad_expand_bias,
    ]
    summed = lax.psum(jnp.concatenate(vectors), "dp")
    pieces, offset = ([], 0)
    for piece in vectors:
        pieces.append(summed[offset : offset + piece.size])
        offset = offset + piece.size
    return (
        jnp.stack(output),
        jnp.stack(grad_tokens),
        jnp.stack(grad_encoded),
        pieces[0],
        pieces[1],
        grad_self_query.astype(F32),
        pieces[9],
        grad_self_key.astype(F32),
        grad_self_value.astype(F32),
        pieces[10],
        grad_self_mixer.astype(F32),
        pieces[2],
        pieces[3],
        pieces[4],
        grad_cross_query.astype(F32),
        pieces[11],
        grad_cross_key.astype(F32),
        grad_cross_value.astype(F32),
        pieces[12],
        grad_cross_mixer.astype(F32),
        pieces[5],
        pieces[6],
        pieces[7],
        grad_expand_weight.astype(F32),
        pieces[13],
        grad_reduce_weight.astype(F32),
        pieces[8],
    )


def solution(mesh):
    rows = P("dp", None, None)
    column, row, part = (P(None, "tensor"), P("tensor", None), P("tensor"))
    return jax.shard_map(
        local,
        mesh=mesh,
        in_specs=(
            rows,
            rows,
            rows,
            P(),
            P(),
            column,
            part,
            column,
            column,
            part,
            row,
            P(),
            P(),
            P(),
            column,
            part,
            column,
            column,
            part,
            row,
            P(),
            P(),
            P(),
            column,
            part,
            row,
            P(),
        ),
        out_specs=(
            rows,
            rows,
            P("dp", None, "tensor"),
            P(),
            P(),
            column,
            part,
            column,
            column,
            part,
            row,
            P(),
            P(),
            P(),
            column,
            part,
            column,
            column,
            part,
            row,
            P(),
            P(),
            P(),
            column,
            part,
            row,
            P(),
        ),
        check_vma=False,
    )
```

profile of v0, /device:TPU:0, one launch (start us, length us, event | category | flops | bytes accessed | tf_op | source)
XLA Modules:
  0.0 1475.0 jit_solution(17825031323830864179)
XLA Ops:
  41.3 9.7 fusion.219
  51.0 8.1 copy_bitcast_fusion
  59.1 4.8 fusion.34
  66.4 4.8 convolution_convert_fusion.3
  81.4 4.7 multiply_reduce_fusion.3
  86.2 5.9 exponential_reduce_fusion.1
  93.5 12.3 fusion.135
  108.2 21.7 %collective-permute-done.1 = bf16[448,1024]{1,0:T(8,128)(2,1)S(1)} collective-permute-done((bf16[448,1024]{1,0:T(8,128)(2,1)S(1)}, bf16[448,1024]{1,0:T(8,128)(2,1)S(1)}, u32[]{:S(2)}, u32[]{:S(2)}) %collective-permute-start.1) | collective-permute-done | bytes 917536 | tf_op jit(solution)/shard_map/ppermute | solution.py:92
  151.8 15.1 %collective-permute-done.6 = bf16[448,1024]{1,0:T(8,128)(2,1)} collective-permute-done((bf16[448,1024]{1,0:T(8,128)(2,1)}, bf16[448,1024]{1,0:T(8,128)(2,1)}, u32[]{:S(2)}, u32[]{:S(2)}) %collective-permute-start.6) | collective-permute-done | bytes 917536 | tf_op jit(solution)/shard_map/ppermute | solution.py:92
  170.5 13.8 collective-permute-done.2
  184.3 4.5 convert_reduce_fusion.4
  194.5 15.2 %multiply_reduce_fusion.1 = (f32[8,448]{1,0:T(8,128)S(1)}, f32[8,448,1500]{2,1,0:T(8,128)}) fusion(f32[8,448,1500]{2,1,0:T(8,128)} %copy-done.1, f32[8,448]{1,0:T(8,128)S(1)} %log_add_fusion.2, bf16[448,8,64]{0,2,1:T(8,128)(2,1)} %bitcast.336, bf16[1500,8,64]{0,2,1:T(8,128)(2,1)} %bitcast.325), kind=kOutput, calls=%fused_computation.3 | convolution fusion | flops 709628416 | bytes 45031424 | tf_op jit(solution)/shard_map/lhe,khe->hlk/dot_general | solution.py:55
  209.7 15.0 %multiply_convert_fusion.1 = bf16[8,448,1500]{2,1,0:T(8,128)(2,1)S(1)} fusion(f32[8,448,1500]{2,1,0:T(8,128)} %get-tuple-element.165, f32[8,448,1500]{2,1,0:T(8,128)} %copy-done.1, f32[8,448]{1,0:T(8,128)S(1)} %get-tuple-element.164, f32[8,448]{1,0:T(8,128)S(1)} %log_add_fusion.2), kind=kLoop, calls=%fused_computation.2 | loop fusion | flops 26880000 | bytes 53788672 | tf_op jit(solution)/shard_map/convert_element_type | solution.py:57
  224.8 4.8 convert_reduce_fusion.9
  241.8 5.5 fusion.222
  247.4 5.9 collective-permute-done.7
  264.9 9.1 multiply_reduce_fusion.5
  274.7 5.3 multiply_convert_fusion.3
  291.1 5.0 fusion.35
  299.1 5.2 collective-permute-done.3
  311.9 4.2 multiply_reduce_fusion.2
  316.1 5.7 exponential_reduce_fusion
  324.0 10.1 fusion.138
  337.3 10.9 convert_reduce_fusion.3
  348.3 6.3 collective-permute-done.4
  374.0 15.8 %collective-permute-done.9 = bf16[448,1024]{1,0:T(8,128)(2,1)S(1)} collective-permute-done((bf16[448,1024]{1,0:T(8,128)(2,1)S(1)}, bf16[448,1024]{1,0:T(8,128)(2,1)S(1)}, u32[]{:S(2)}, u32[]{:S(2)}) %collective-permute-start.9) | collective-permute-done | bytes 917536 | tf_op jit(solution)/shard_map/ppermute | solution.py:92
  391.3 12.4 collective-permute-done.5
  416.4 11.9 convert_reduce_fusion.2
  429.6 5.4 fusion.113
  435.0 15.4 %multiply_reduce_fusion = (f32[8,448]{1,0:T(8,128)S(1)}, f32[8,448,1500]{2,1,0:T(8,128)}) fusion(f32[8,448,1500]{2,1,0:T(8,128)} %copy-done.2, f32[8,448]{1,0:T(8,128)S(1)} %log_add_fusion, bf16[448,8,64]{0,2,1:T(8,128)(2,1)} %bitcast.339, bf16[1500,8,64]{0,2,1:T(8,128)(2,1)} %bitcast.322), kind=kOutput, calls=%fused_computation.1 | convolution fusion | flops 709628416 | bytes 45031424 | tf_op jit(solution)/shard_map/lhe,khe->hlk/dot_general | solution.py:55
  450.9 14.9 %multiply_convert_fusion = bf16[8,448,1500]{2,1,0:T(8,128)(2,1)S(1)} fusion(f32[8,448,1500]{2,1,0:T(8,128)} %get-tuple-element.172, f32[8,448,1500]{2,1,0:T(8,128)} %copy-done.2, f32[8,448]{1,0:T(8,128)S(1)} %get-tuple-element.171, f32[8,448]{1,0:T(8,128)S(1)} %log_add_fusion), kind=kLoop, calls=%fused_computation | loop fusion | flops 26880000 | bytes 53788672 | tf_op jit(solution)/shard_map/convert_element_type | solution.py:57
  473.7 5.4 fusion.110
  479.2 8.1 convert_reduce_fusion.8
  490.6 5.9 convert_reduce_fusion.11
  499.3 6.6 collective-permute-done.10
  513.9 5.3 convert_reduce_fusion.10
  528.0 4.7 multiply_reduce_fusion.4
  532.7 4.2 multiply_convert_fusion.2
  552.2 6.2 convolution_convert_fusion
  559.8 8.2 convolution_convert_fusion.1
  569.4 23.4 %reduce-scatter.21.cloned.1.call-done = bf16[64,512]{1,0:T(8,128)(2,1)} async-done(((bf16[1024,512]{1,0:T(8,128)(2,1)}), bf16[64,512]{1,0:T(8,128)(2,1)}) %reduce-scatter.21.cloned.1.call-update) | async-done | bytes 65552 | tf_op jit(solution)/shard_map/reduce_scatter | solution.py:97
  592.8 60.1 %reduce-scatter.19.cloned.1.call-done = bf16[64,512]{1,0:T(8,128)(2,1)} async-done(((bf16[1024,512]{1,0:T(8,128)(2,1)}), bf16[64,512]{1,0:T(8,128)(2,1)}) %reduce-scatter.19.cloned.1.call-update) | async-done | bytes 65552 | tf_op jit(solution)/shard_map/reduce_scatter | solution.py:97
  652.9 60.1 %reduce-scatter.15.cloned.1.call-done = bf16[64,512]{1,0:T(8,128)(2,1)} async-done(((bf16[1024,512]{1,0:T(8,128)(2,1)}), bf16[64,512]{1,0:T(8,128)(2,1)}) %reduce-scatter.15.cloned.1.call-update) | async-done | bytes 65552 | tf_op jit(solution)/shard_map/reduce_scatter | solution.py:97
  713.1 60.1 %reduce-scatter.17.cloned.1.call-done = bf16[32,1024]{1,0:T(8,128)(2,1)} async-done(((bf16[512,1024]{1,0:T(8,128)(2,1)}), bf16[32,1024]{1,0:T(8,128)(2,1)}) %reduce-scatter.17.cloned.1.call-update) | async-done | bytes 65552 | tf_op jit(solution)/shard_map/reduce_scatter | solution.py:97
  773.2 60.8 %reduce-scatter.11.cloned.1.call-done = bf16[64,512]{1,0:T(8,128)(2,1)} async-done(((bf16[1024,512]{1,0:T(8,128)(2,1)}), bf16[64,512]{1,0:T(8,128)(2,1)}) %reduce-scatter.11.cloned.1.call-update) | async-done | bytes 65552 | tf_op jit(solution)/shard_map/reduce_scatter | solution.py:97
  834.1 60.7 %reduce-scatter.13.cloned.1.call-done = bf16[64,512]{1,0:T(8,128)(2,1)} async-done(((bf16[1024,512]{1,0:T(8,128)(2,1)}), bf16[64,512]{1,0:T(8,128)(2,1)}) %reduce-scatter.13.cloned.1.call-update) | async-done | bytes 65552 | tf_op jit(solution)/shard_map/reduce_scatter | solution.py:97
  894.9 76.2 %reduce-scatter.29.cloned.1.call-done = bf16[128,1024]{1,0:T(8,128)(2,1)} async-done(((bf16[2048,1024]{1,0:T(8,128)(2,1)}), bf16[128,1024]{1,0:T(8,128)(2,1)}) %reduce-scatter.29.cloned.1.call-update) | async-done | bytes 262160 | tf_op jit(solution)/shard_map/reduce_scatter | solution.py:97
  983.4 29.0 %collective-permute-done.12 = bf16[1500,512]{1,0:T(8,128)(2,1)} collective-permute-done((bf16[1500,512]{1,0:T(8,128)(2,1)}, bf16[1500,512]{1,0:T(8,128)(2,1)}, u32[]{:S(2)}, u32[]{:S(2)}) %collective-permute-start.12) | collective-permute-done | bytes 1536032 | tf_op jit(solution)/shard_map/ppermute | solution.py:294
  1012.4 4.2 add_bitcast_fusion.1
  1019.2 28.0 %reduce-scatter.27.cloned.1.call-done = bf16[64,2048]{1,0:T(8,128)(2,1)} async-done(((bf16[1024,2048]{1,0:T(8,128)(2,1)}), bf16[64,2048]{1,0:T(8,128)(2,1)}) %reduce-scatter.27.cloned.1.call-update) | async-done | bytes 262160 | tf_op jit(solution)/shard_map/reduce_scatter | solution.py:97
  1047.3 4.7 fusion.37
  1063.9 25.0 %collective-permute-done.13 = bf16[1500,512]{1,0:T(8,128)(2,1)} collective-permute-done((bf16[1500,512]{1,0:T(8,128)(2,1)}, bf16[1500,512]{1,0:T(8,128)(2,1)}, u32[]{:S(2)}, u32[]{:S(2)}) %collective-permute-start.13) | collective-permute-done | bytes 1536032 | tf_op jit(solution)/shard_map/ppermute | solution.py:294
  1093.7 12.7 copy.122
  1106.5 4.0 fusion.70
  1110.9 57.9 %psum.7 = f32[13312]{0:T(1024)S(1)} all-reduce(f32[13312]{0:T(1024)S(1)} %add_dynamic-update-slice_fusion), channel_id=1, replica_groups=mesh['dp'=16,'tensor'=2] {'dp'}, use_global_device_ids=true, to_apply=%region_64.65 | all-reduce | flops 13312 | bytes 106496 | tf_op jit(solution)/shard_map/psum | solution.py:327
  1185.3 17.9 %all-gather.19.cloned.1.call-done = bf16[1024,512]{1,0:T(8,128)(2,1)} async-done(((bf16[64,512]{1,0:T(8,128)(2,1)}), bf16[1024,512]{1,0:T(8,128)(2,1)}) %all-gather.19.cloned.1.call-update) | async-done | bytes 1048592 | tf_op jit(solution)/shard_map/all_gather | solution.py:98
  1206.1 36.0 %all-gather.15.cloned.1.call-done = bf16[1024,512]{1,0:T(8,128)(2,1)} async-done(((bf16[64,512]{1,0:T(8,128)(2,1)}), bf16[1024,512]{1,0:T(8,128)(2,1)}) %all-gather.15.cloned.1.call-update) | async-done | bytes 1048592 | tf_op jit(solution)/shard_map/all_gather | solution.py:98
  1245.0 36.0 %all-gather.17.cloned.1.call-done = bf16[512,1024]{1,0:T(8,128)(2,1)} async-done(((bf16[32,1024]{1,0:T(8,128)(2,1)}), bf16[512,1024]{1,0:T(8,128)(2,1)}) %all-gather.17.cloned.1.call-update) | async-done | bytes 1048592 | tf_op jit(solution)/shard_map/all_gather | solution.py:98
  1283.8 36.1 %all-gather.11.cloned.1.call-done = bf16[1024,512]{1,0:T(8,128)(2,1)} async-done(((bf16[64,512]{1,0:T(8,128)(2,1)}), bf16[1024,512]{1,0:T(8,128)(2,1)}) %all-gather.11.cloned.1.call-update) | async-done | bytes 1048592 | tf_op jit(solution)/shard_map/all_gather | solution.py:98
  1322.8 36.0 %all-gather.13.cloned.1.call-done = bf16[1024,512]{1,0:T(8,128)(2,1)} async-done(((bf16[64,512]{1,0:T(8,128)(2,1)}), bf16[1024,512]{1,0:T(8,128)(2,1)}) %all-gather.13.cloned.1.call-update) | async-done | bytes 1048592 | tf_op jit(solution)/shard_map/all_gather | solution.py:98
  1361.6 48.7 %all-gather.29.cloned.1.call-done = bf16[2048,1024]{1,0:T(8,128)(2,1)} async-done(((bf16[128,1024]{1,0:T(8,128)(2,1)}), bf16[2048,1024]{1,0:T(8,128)(2,1)}) %all-gather.29.cloned.1.call-update) | async-done | bytes 4194320 | tf_op jit(solution)/shard_map/all_gather | solution.py:98
  1410.3 6.6 convert_element_type.662
  1417.0 44.3 %all-gather.27.cloned.1.call-done = bf16[1024,2048]{1,0:T(8,128)(2,1)} async-done(((bf16[64,2048]{1,0:T(8,128)(2,1)}), bf16[1024,2048]{1,0:T(8,128)(2,1)}) %all-gather.27.cloned.1.call-update) | async-done | bytes 4194320 | tf_op jit(solution)/shard_map/all_gather | solution.py:98
  1461.3 6.7 convert_element_type.660
  (591 shorter events, 279.0 us)
Async XLA Ops:
  7.2 59.2 %copy-start = (bf16[1024,512]{1,0:T(8,128)(2,1)S(1)}, bf16[1024,512]{1,0:T(8,128)(2,1)}, u32[]{:S(2)}) copy-start(bf16[1024,512]{1,0:T(8,128)(2,1)} %param.43) | copy-start | bytes 3145732
  7.2 560.9 %reduce-scatter.25.cloned.1.call-start = ((), (), s32[]{:S(2)}) async-start(), calls=%async_computation.24 | async-start | bytes 1114112 | tf_op jit(solution)/shard_map/reduce_scatter | solution.py:97
  36.5 14.5 copy-start.155
  38.2 35.6 %collective-permute-start = (bf16[448,1024]{1,0:T(8,128)(2,1)}, bf16[448,1024]{1,0:T(8,128)(2,1)}, u32[]{:S(2)}, u32[]{:S(2)}) collective-permute-start(bf16[448,1024]{1,0:T(8,128)(2,1)} %convolution_convert_fusion.14), channel_id=1, source_target_pairs={{0,1},{1,0},{2,3},{3,2},{4,5},{5,4},{6,7},{7,6},{8,9},{9,8},{10,11... | collective-permute-start | bytes 2752520 | tf_op jit(solution)/shard_map/ppermute | solution.py:92
  105.9 24.1 %copy-start.11 = (f32[448,1024]{1,0:T(8,128)S(1)}, f32[448,1024]{1,0:T(8,128)}, u32[]{:S(2)}) copy-start(f32[448,1024]{1,0:T(8,128)} %copy-done.10) | copy-start | bytes 5505028
  108.1 21.9 %collective-permute-start.1 = (bf16[448,1024]{1,0:T(8,128)(2,1)S(1)}, bf16[448,1024]{1,0:T(8,128)(2,1)S(1)}, u32[]{:S(2)}, u32[]{:S(2)}) collective-permute-start(bf16[448,1024]{1,0:T(8,128)(2,1)S(1)} %convolution_convert_fusion.13), channel_id=1, source_target_pairs={{0,1},{1,0},{2,3},{3,2},{4,5},{5,4},{6,7},{7,6},{8,9},{9,8},{10,11... | collective-permute-start | bytes 2752520 | tf_op jit(solution)/shard_map/ppermute | solution.py:92
  143.3 23.5 %collective-permute-start.6 = (bf16[448,1024]{1,0:T(8,128)(2,1)}, bf16[448,1024]{1,0:T(8,128)(2,1)}, u32[]{:S(2)}, u32[]{:S(2)}) collective-permute-start(bf16[448,1024]{1,0:T(8,128)(2,1)} %convolution_convert_fusion.16), channel_id=1, source_target_pairs={{0,1},{1,0},{2,3},{3,2},{4,5},{5,4},{6,7},{7,6},{8,9},{9,8},{10,11... | collective-permute-start | bytes 2752520 | tf_op jit(solution)/shard_map/ppermute | solution.py:92
  146.6 37.6 %collective-permute-start.2 = (bf16[448,1024]{1,0:T(8,128)(2,1)}, bf16[448,1024]{1,0:T(8,128)(2,1)}, u32[]{:S(2)}, u32[]{:S(2)}) collective-permute-start(bf16[448,1024]{1,0:T(8,128)(2,1)} %convolution_convert_fusion.18), channel_id=1, source_target_pairs={{0,1},{1,0},{2,3},{3,2},{4,5},{5,4},{6,7},{7,6},{8,9},{9,8},{10,11... | collective-permute-start | bytes 2752520 | tf_op jit(solution)/shard_map/ppermute | solution.py:92
  151.8 32.5 %copy-start.14 = (f32[448,1024]{1,0:T(8,128)S(1)}, f32[448,1024]{1,0:T(8,128)}, u32[]{:S(2)}) copy-start(f32[448,1024]{1,0:T(8,128)} %copy-done.13) | copy-start | bytes 5505028
  151.8 32.5 %copy-start.37 = (bf16[2,448,1024]{2,1,0:T(8,128)(2,1)S(1)}, bf16[2,448,1024]{2,1,0:T(8,128)(2,1)}, u32[]{:S(2)}) copy-start(bf16[2,448,1024]{2,1,0:T(8,128)(2,1)} %param.29) | copy-start | bytes 5505028
  209.7 15.0 %copy-start.22 = (bf16[1500,512]{0,1:T(8,128)(2,1)S(1)}, bf16[1500,512]{0,1:T(8,128)(2,1)}, u32[]{:S(2)}) copy-start(bf16[1500,512]{0,1:T(8,128)(2,1)} %copy.103) | copy-start | bytes 4608004
  232.9 20.4 %collective-permute-start.7 = (bf16[448,1024]{1,0:T(8,128)(2,1)}, bf16[448,1024]{1,0:T(8,128)(2,1)}, u32[]{:S(2)}, u32[]{:S(2)}) collective-permute-start(bf16[448,1024]{1,0:T(8,128)(2,1)} %convolution_convert_fusion.10), channel_id=1, source_target_pairs={{0,1},{1,0},{2,3},{3,2},{4,5},{5,4},{6,7},{7,6},{8,9},{9,8},{10,11... | collective-permute-start | bytes 2752520 | tf_op jit(solution)/shard_map/ppermute | solution.py:92
  241.8 11.5 copy-start.12
  247.4 9.0 copy-start.28
  264.9 9.1 slice-start
  264.9 9.1 slice-start.2
  264.9 9.1 slice-start.1
  264.9 9.7 slice-start.3
  284.8 19.5 %collective-permute-start.3 = (bf16[448,1024]{1,0:T(8,128)(2,1)}, bf16[448,1024]{1,0:T(8,128)(2,1)}, u32[]{:S(2)}, u32[]{:S(2)}) collective-permute-start(bf16[448,1024]{1,0:T(8,128)(2,1)} %convolution_convert_fusion.12), channel_id=1, source_target_pairs={{0,1},{1,0},{2,3},{3,2},{4,5},{5,4},{6,7},{7,6},{8,9},{9,8},{10,11... | collective-permute-start | bytes 2752520 | tf_op jit(solution)/shard_map/ppermute | solution.py:92
  336.2 18.5 %copy-start.9 = (f32[448,1024]{1,0:T(8,128)S(1)}, f32[448,1024]{1,0:T(8,128)}, u32[]{:S(2)}) copy-start(f32[448,1024]{1,0:T(8,128)} %copy-done.8) | copy-start | bytes 5505028
  336.2 18.4 %collective-permute-start.4 = (bf16[448,1024]{1,0:T(8,128)(2,1)S(1)}, bf16[448,1024]{1,0:T(8,128)(2,1)S(1)}, u32[]{:S(2)}, u32[]{:S(2)}) collective-permute-start(bf16[448,1024]{1,0:T(8,128)(2,1)S(1)} %convolution_convert_fusion.11), channel_id=1, source_target_pairs={{0,1},{1,0},{2,3},{3,2},{4,5},{5,4},{6,7},{7,6},{8,9},{9,8},{10,11... | collective-permute-start | bytes 2752520 | tf_op jit(solution)/shard_map/ppermute | solution.py:92
  366.5 23.3 %collective-permute-start.9 = (bf16[448,1024]{1,0:T(8,128)(2,1)S(1)}, bf16[448,1024]{1,0:T(8,128)(2,1)S(1)}, u32[]{:S(2)}, u32[]{:S(2)}) collective-permute-start(bf16[448,1024]{1,0:T(8,128)(2,1)S(1)} %convolution_convert_fusion.15), channel_id=1, source_target_pairs={{0,1},{1,0},{2,3},{3,2},{4,5},{5,4},{6,7},{7,6},{8,9},{9,8},{10,11... | collective-permute-start | bytes 2752520 | tf_op jit(solution)/shard_map/ppermute | solution.py:92
  370.0 33.7 %collective-permute-start.5 = (bf16[448,1024]{1,0:T(8,128)(2,1)S(1)}, bf16[448,1024]{1,0:T(8,128)(2,1)S(1)}, u32[]{:S(2)}, u32[]{:S(2)}) collective-permute-start(bf16[448,1024]{1,0:T(8,128)(2,1)S(1)} %convolution_convert_fusion.17), channel_id=1, source_target_pairs={{0,1},{1,0},{2,3},{3,2},{4,5},{5,4},{6,7},{7,6},{8,9},{9,8},{10,11... | collective-permute-start | bytes 2752520 | tf_op jit(solution)/shard_map/ppermute | solution.py:92
  414.1 154.7 %reduce-scatter.23.cloned.1.call-start = ((), (), s32[]{:S(2)}) async-start(), calls=%async_computation.22 | async-start | bytes 1114112 | tf_op jit(solution)/shard_map/reduce_scatter | solution.py:97
  416.4 13.1 copy-start.30
  416.4 13.1 copy-start.62
  416.4 13.1 copy-start.64
  450.4 142.3 %reduce-scatter.21.cloned.1.call-start = ((), (), s32[]{:S(2)}) async-start(), calls=%async_computation.20 | async-start | bytes 1114112 | tf_op jit(solution)/shard_map/reduce_scatter | solution.py:97
  450.9 15.0 %copy-start.41 = (bf16[448,512]{0,1:T(8,128)(2,1)S(1)}, bf16[448,512]{0,1:T(8,128)(2,1)}, u32[]{:S(2)}) copy-start(bf16[448,512]{0,1:T(8,128)(2,1)} %copy.110) | copy-start | bytes 1376260
  479.1 173.8 %reduce-scatter.19.cloned.1.call-start = ((), (), s32[]{:S(2)}) async-start(), calls=%async_computation.18 | async-start | bytes 1114112 | tf_op jit(solution)/shard_map/reduce_scatter | solution.py:97
  489.0 16.9 %collective-permute-start.10 = (bf16[448,1024]{1,0:T(8,128)(2,1)}, bf16[448,1024]{1,0:T(8,128)(2,1)}, u32[]{:S(2)}, u32[]{:S(2)}) collective-permute-start(bf16[448,1024]{1,0:T(8,128)(2,1)} %convolution_convert_fusion.9), channel_id=1, source_target_pairs={{0,1},{1,0},{2,3},{3,2},{4,5},{5,4},{6,7},{7,6},{8,9},{9,8},{10,11... | collective-permute-start | bytes 2752520 | tf_op jit(solution)/shard_map/ppermute | solution.py:92
  499.1 214.0 %reduce-scatter.15.cloned.1.call-start = ((), (), s32[]{:S(2)}) async-start(), calls=%async_computation.14 | async-start | bytes 1114112 | tf_op jit(solution)/shard_map/reduce_scatter | solution.py:97
  499.3 9.1 copy-start.26
  522.5 250.7 %reduce-scatter.17.cloned.1.call-start = ((), (), s32[]{:S(2)}) async-start(), calls=%async_computation.16 | async-start | bytes 1114112 | tf_op jit(solution)/shard_map/reduce_scatter | solution.py:97
  525.6 13.2 copy-start.73
  527.9 306.1 %reduce-scatter.11.cloned.1.call-start = ((), (), s32[]{:S(2)}) async-start(), calls=%async_computation.10 | async-start | bytes 1114112 | tf_op jit(solution)/shard_map/reduce_scatter | solution.py:97
  542.2 352.6 %reduce-scatter.13.cloned.1.call-start = ((), (), s32[]{:S(2)}) async-start(), calls=%async_computation.12 | async-start | bytes 1114112 | tf_op jit(solution)/shard_map/reduce_scatter | solution.py:97
  550.0 421.1 %reduce-scatter.29.cloned.1.call-start = ((), (), s32[]{:S(2)}) async-start(), calls=%async_computation.28 | async-start | bytes 4456448 | tf_op jit(solution)/shard_map/reduce_scatter | solution.py:97
  558.4 488.8 %reduce-scatter.27.cloned.1.call-start = ((), (), s32[]{:S(2)}) async-start(), calls=%async_computation.26 | async-start | bytes 4456448 | tf_op jit(solution)/shard_map/reduce_scatter | solution.py:97
  568.0 403.6 %copy-start.18 = (bf16[8,64,1500]{2,1,0:T(8,128)(2,1)S(1)}, bf16[8,64,1500]{2,1,0:T(8,128)(2,1)}, u32[]{:S(2)}) copy-start(bf16[8,64,1500]{2,1,0:T(8,128)(2,1)} %fusion.32) | copy-start | bytes 4608004
  568.0 608.8 %all-gather.25.cloned.1.call-start = ((), (), s32[]{:S(2)}) async-start(), calls=%async_computation.25 | async-start | bytes 1114112 | tf_op jit(solution)/shard_map/all_gather | solution.py:98
  568.8 610.9 %all-gather.23.cloned.1.call-start = ((), (), s32[]{:S(2)}) async-start(), calls=%async_computation.23 | async-start | bytes 1114112 | tf_op jit(solution)/shard_map/all_gather | solution.py:98
  569.3 613.2 %all-gather.21.cloned.1.call-start = ((), (), s32[]{:S(2)}) async-start(), calls=%async_computation.21 | async-start | bytes 1114112 | tf_op jit(solution)/shard_map/all_gather | solution.py:98
  592.8 610.5 %all-gather.19.cloned.1.call-start = ((), (), s32[]{:S(2)}) async-start(), calls=%async_computation.19 | async-start | bytes 1114112 | tf_op jit(solution)/shard_map/all_gather | solution.py:98
  652.9 589.3 %all-gather.15.cloned.1.call-start = ((), (), s32[]{:S(2)}) async-start(), calls=%async_computation.15 | async-start | bytes 1114112 | tf_op jit(solution)/shard_map/all_gather | solution.py:98
  713.0 568.0 %all-gather.17.cloned.1.call-start = ((), (), s32[]{:S(2)}) async-start(), calls=%async_computation.17 | async-start | bytes 1114112 | tf_op jit(solution)/shard_map/all_gather | solution.py:98
  773.2 546.7 %all-gather.11.cloned.1.call-start = ((), (), s32[]{:S(2)}) async-start(), calls=%async_computation.11 | async-start | bytes 1114112 | tf_op jit(solution)/shard_map/all_gather | solution.py:98
  834.0 524.8 %all-gather.13.cloned.1.call-start = ((), (), s32[]{:S(2)}) async-start(), calls=%async_computation.13 | async-start | bytes 1114112 | tf_op jit(solution)/shard_map/all_gather | solution.py:98
  894.8 515.5 %all-gather.29.cloned.1.call-start = ((), (), s32[]{:S(2)}) async-start(), calls=%async_computation.29 | async-start | bytes 4456448 | tf_op jit(solution)/shard_map/all_gather | solution.py:98
  971.1 490.2 %all-gather.27.cloned.1.call-start = ((), (), s32[]{:S(2)}) async-start(), calls=%async_computation.27 | async-start | bytes 4456448 | tf_op jit(solution)/shard_map/all_gather | solution.py:98
  975.5 36.9 %collective-permute-start.12 = (bf16[1500,512]{1,0:T(8,128)(2,1)}, bf16[1500,512]{1,0:T(8,128)(2,1)}, u32[]{:S(2)}, u32[]{:S(2)}) collective-permute-start(bf16[1500,512]{1,0:T(8,128)(2,1)} %fusion.36), channel_id=1, source_target_pairs={{0,1},{1,0},{2,3},{3,2},{4,5},{5,4},{6,7},{7,6},{8,9},{9,8},{10,11... | collective-permute-start | bytes 4608008 | tf_op jit(solution)/shard_map/ppermute | solution.py:294
  981.1 31.3 %copy-start.32 = (bf16[8,64,1500]{2,1,0:T(8,128)(2,1)S(1)}, bf16[8,64,1500]{2,1,0:T(8,128)(2,1)}, u32[]{:S(2)}) copy-start(bf16[8,64,1500]{2,1,0:T(8,128)(2,1)} %get-tuple-element.188) | copy-start | bytes 4608004
  981.1 31.3 %copy-start.60 = (bf16[1024,512]{1,0:T(8,128)(2,1)S(1)}, bf16[1024,512]{1,0:T(8,128)(2,1)}, u32[]{:S(2)}) copy-start(bf16[1024,512]{1,0:T(8,128)(2,1)} %param.44) | copy-start | bytes 3145732
  982.8 33.7 %copy-start.20 = (bf16[8,64,1500]{2,1,0:T(8,128)(2,1)S(1)}, bf16[8,64,1500]{2,1,0:T(8,128)(2,1)}, u32[]{:S(2)}) copy-start(bf16[8,64,1500]{2,1,0:T(8,128)(2,1)} %copy-done.19) | copy-start | bytes 4608004
  982.8 123.6 %collective-permute-start.8 = (bf16[448,1024]{1,0:T(8,128)(2,1)}, bf16[448,1024]{1,0:T(8,128)(2,1)}, u32[]{:S(2)}, u32[]{:S(2)}) collective-permute-start(bf16[448,1024]{1,0:T(8,128)(2,1)} %add_convert_fusion.1), channel_id=1, source_target_pairs={{0,1},{1,0},{2,3},{3,2},{4,5},{5,4},{6,7},{7,6},{8,9},{9,8},{10,11... | collective-permute-start | bytes 2752520 | tf_op jit(solution)/shard_map/ppermute | solution.py:92
  1052.0 36.9 %collective-permute-start.13 = (bf16[1500,512]{1,0:T(8,128)(2,1)}, bf16[1500,512]{1,0:T(8,128)(2,1)}, u32[]{:S(2)}, u32[]{:S(2)}) collective-permute-start(bf16[1500,512]{1,0:T(8,128)(2,1)} %fusion.37), channel_id=1, source_target_pairs={{0,1},{1,0},{2,3},{3,2},{4,5},{5,4},{6,7},{7,6},{8,9},{9,8},{10,11... | collective-permute-start | bytes 4608008 | tf_op jit(solution)/shard_map/ppermute | solution.py:294
  1060.7 45.8 %collective-permute-start.11 = (bf16[448,1024]{1,0:T(8,128)(2,1)}, bf16[448,1024]{1,0:T(8,128)(2,1)}, u32[]{:S(2)}, u32[]{:S(2)}) collective-permute-start(bf16[448,1024]{1,0:T(8,128)(2,1)} %add_convert_fusion), channel_id=1, source_target_pairs={{0,1},{1,0},{2,3},{3,2},{4,5},{5,4},{6,7},{7,6},{8,9},{9,8},{10,11... | collective-permute-start | bytes 2752520 | tf_op jit(solution)/shard_map/ppermute | solution.py:92
  1061.3 27.6 %copy-start.34 = (bf16[8,64,1500]{2,1,0:T(8,128)(2,1)S(1)}, bf16[8,64,1500]{2,1,0:T(8,128)(2,1)}, u32[]{:S(2)}) copy-start(bf16[8,64,1500]{2,1,0:T(8,128)(2,1)} %copy-done.33) | copy-start | bytes 4608004
  1093.6 12.9 copy-start.7
  1093.6 12.9 copy-start.109
  1093.6 12.9 copy-start.111
  1093.6 12.9 copy-start.113
  1093.7 12.9 copy-start.115
  1093.7 12.9 copy-start.117
  (144 other events, 470.6 us)
Sparse Core Ops, SparseCore 0:
  414.3 57.9 reduce-scatter.24
  475.8 56.7 reduce-scatter.22
  536.3 56.4 reduce-scatter.20
  596.2 56.6 reduce-scatter.18
  656.3 56.6 reduce-scatter.14
  716.5 56.6 reduce-scatter.16
  777.4 56.6 reduce-scatter.10
  838.2 56.5 reduce-scatter.12
  899.2 71.8 reduce-scatter.28
  975.4 71.8 reduce-scatter.26
  1049.4 36.9 all-gather.24
  1088.4 36.8 all-gather.22
  1127.5 36.8 all-gather.20
  1166.4 36.7 all-gather.18
  1205.3 36.8 all-gather.14
  1244.2 36.8 all-gather.16
  1283.1 36.8 all-gather.10
  1321.9 36.8 all-gather.12
  1361.0 49.3 all-gather.28
  1412.4 48.8 all-gather.26
where the time goes:
time: 1480 us; the launch traced here: 1470 us
  waiting for transfers between devices  843 us (57%)
  matrix products  294 us (20%)
  other arithmetic  140 us (9%)
  local copies, waits for them, and re-layouts  105 us (7%)
  blocking collectives  57.9 us (4%)
  starting transfers between devices  17.7 us (1%)
  between operations  16.5 us (1%)
    reduce_scatter x10, waiting for transfers between devices, dp_sum(): share = lax.psum_scatter(grads, 'dp', scatter_dimension=0, tiled=True)  429 us
    all_gather x10, waiting for transfers between devices, dp_sum(): return lax.all_gather(share, 'dp', axis=0, tiled=True)  255 us
    ppermute x12, waiting for transfers between devices, tensor_sum(): other = lax.ppermute(mine, 'tensor', [(0, 1), (1, 0)])  103 us
    psum x1, blocking collectives, local(): summed = lax.psum(jnp.concatenate(vectors), 'dp')  57.9 us
    ppermute x2, waiting for transfers between devices, local(): other = lax.ppermute(terms(1 - me).astype(BF16), 'tensor', [(0, 1), (1, 0)])  54 us
    dot_general x24, matrix products, project_back(): return jnp.einsum('lc,dc->ld', grads, weight, preferred_element_type=F32)  53.9 us
    unnamed x353, local copies, waits for them, and re-layouts  52.1 us
    dot_general x20, matrix products, project(): return jnp.dot(inputs, weight, preferred_element_type=F32)  51.3 us
  transfers between devices with their start and end apart: 34, of which 26 were waited for; matrix products, arithmetic and copies ran while one was open for 20% of the time, Pallas kernels for 0%

commit v1 on v0

--- a/solution.py
+++ b/solution.py
@@ -1,3 +1,4 @@
+import functools
 import math
 import jax
 import jax.numpy as jnp
@@ -8,6 +9,34 @@
 EPSILON = 1e-05
 F32 = jnp.float32
 BF16 = jnp.bfloat16
+
+
+def supply_teams(mat, dim_no):
+    raw_out = list(mat.shape[1:])
+    raw_out[dim_no] *= mat.shape[0]
+    side_arr = jnp.moveaxis(mat, 0, dim_no).reshape(raw_out)
+    return side_arr
+
+
+def body_wait(own_rows, shard_axis):
+    now, big = (lax.axis_size(shard_axis), lax.axis_index(shard_axis))
+    view_out, long_array = (own_rows[None], 1)
+    while long_array < now:
+        val = lax.ppermute(view_out, shard_axis, [(kk, kk ^ long_array) for kk in range(now)])
+        passed = big & long_array == 0
+        view_out = jnp.concatenate(
+            [jnp.where(passed, view_out, val), jnp.where(passed, val, view_out)]
+        )
+        long_array *= 2
+    return view_out
+
+
+def panels_make(u_in, x0, where_dim):
+    v1 = supply_teams(body_wait(u_in, x0), where_dim)
+    return v1
+
+
+trace_the_sources_all = functools.partial(panels_make, x0="dp", where_dim=0)
 
 
 def normalize(values, norm_gain, norm_shift):
@@ -95,7 +124,7 @@
 
 def dp_sum(grads):
     share = lax.psum_scatter(grads, "dp", scatter_dimension=0, tiled=True)
-    return lax.all_gather(share, "dp", axis=0, tiled=True)
+    return trace_the_sources_all(share)
 
 
 def local(

time: 1480 us -> 1420 us (0.959)
  waiting for transfers between devices: 843 us -> 695 us
  starting transfers between devices: 17.7 us -> 54.9 us
  other arithmetic: 140 us -> 173 us
    all_gather x10 -> x0, waiting for transfers between devices: 255 us -> none  [dp_sum(): return lax.all_gather(share, 'dp', axis=0, tiled=True)]
    ppermute x0 -> x40, waiting for transfers between devices: none -> 233 us  [body_wait(): lax.ppermute(view_out, shard_axis, [(kk, kk ^ long_array) for kk in range...]
    reduce_scatter x10, waiting for transfers between devices: 429 us -> 304 us  [dp_sum(): share = lax.psum_scatter(grads, 'dp', scatter_dimension=0, tiled=True)]
    ppermute x0 -> x40, starting transfers between devices: none -> 37.5 us  [body_wait(): lax.ppermute(view_out, shard_axis, [(kk, kk ^ long_array) for kk in range...]
    select_n x0 -> x40, other arithmetic: none -> 20.6 us  [body_wait(): jnp.where(passed, view_out, val)]
    unnamed x353 -> x397, local copies, waits for them, and re-layouts: 52.1 us -> 58.3 us
  transfers between devices with their start and end apart: 34 -> 64, of which waited for: 26 -> 29; matrix products, arithmetic and copies ran while one was open for 20% -> 24% of each run, Pallas kernels for 0% -> 0%
where the time goes in v1:
time: 1420 us; the launch traced here: 1410 us
  waiting for transfers between devices  695 us (49%)
  matrix products  294 us (21%)
  other arithmetic  173 us (12%)
  local copies, waits for them, and re-layouts  114 us (8%)
  blocking collectives  61.2 us (4%)
  starting transfers between devices  54.9 us (4%)
  between operations  16.9 us (1%)
    reduce_scatter x10, waiting for transfers between devices, dp_sum(): share = lax.psum_scatter(grads, 'dp', scatter_dimension=0, tiled=True)  304 us
    ppermute x40, waiting for transfers between devices, body_wait(): lax.ppermute(view_out, shard_axis, [(kk, kk ^ long_array) for kk in range...  233 us
    ppermute x12, waiting for transfers between devices, tensor_sum(): other = lax.ppermute(mine, 'tensor', [(0, 1), (1, 0)])  106 us
    psum x1, blocking collectives, local(): summed = lax.psum(jnp.concatenate(vectors), 'dp')  61.2 us
    unnamed x397, local copies, waits for them, and re-layouts  58.3 us
    dot_general x24, matrix products, project_back(): return jnp.einsum('lc,dc->ld', grads, weight, preferred_element_type=F32)  52.9 us
    dot_general x20, matrix products, project(): return jnp.dot(inputs, weight, preferred_element_type=F32)  51.3 us
    ppermute x2, waiting for transfers between devices, local(): other = lax.ppermute(terms(1 - me).astype(BF16), 'tensor', [(0, 1), (1, 0)])  51.1 us
  transfers between devices with their start and end apart: 64, of which 29 were waited for; matrix products, arithmetic and copies ran while one was open for 24% of the time, Pallas kernels for 0%

profile of v1, /device:TPU:0, one launch (start us, length us, event | category | flops | bytes accessed | tf_op | source)
XLA Modules:
  0.0 1407.6 jit_solution(3977421016702597206)
XLA Ops:
  41.5 9.8 fusion.219
  51.3 8.0 copy_bitcast_fusion
  59.3 4.8 fusion.34
  66.6 4.8 convolution_convert_fusion.3
  81.5 4.7 multiply_reduce_fusion.3
  86.3 6.1 exponential_reduce_fusion.1
  93.6 12.4 fusion.135
  108.4 21.7 %collective-permute-done.1 = bf16[448,1024]{1,0:T(8,128)(2,1)S(1)} collective-permute-done((bf16[448,1024]{1,0:T(8,128)(2,1)S(1)}, bf16[448,1024]{1,0:T(8,128)(2,1)S(1)}, u32[]{:S(2)}, u32[]{:S(2)}) %collective-permute-start.1) | collective-permute-done | bytes 917536 | tf_op jit(solution)/shard_map/ppermute | solution.py:121
  136.5 4.0 convert_reduce_fusion.1
  151.9 15.1 %collective-permute-done.6 = bf16[448,1024]{1,0:T(8,128)(2,1)} collective-permute-done((bf16[448,1024]{1,0:T(8,128)(2,1)}, bf16[448,1024]{1,0:T(8,128)(2,1)}, u32[]{:S(2)}, u32[]{:S(2)}) %collective-permute-start.6) | collective-permute-done | bytes 917536 | tf_op jit(solution)/shard_map/ppermute | solution.py:121
  167.0 3.6 multiply_reduce_fusion.7
  170.6 13.8 collective-permute-done.2
  184.4 4.5 convert_reduce_fusion.4
  194.6 15.2 %multiply_reduce_fusion.1 = (f32[8,448]{1,0:T(8,128)S(1)}, f32[8,448,1500]{2,1,0:T(8,128)}) fusion(f32[8,448,1500]{2,1,0:T(8,128)} %copy-done.1, f32[8,448]{1,0:T(8,128)S(1)} %log_add_fusion.2, bf16[448,8,64]{0,2,1:T(8,128)(2,1)} %bitcast.396, bf16[1500,8,64]{0,2,1:T(8,128)(2,1)} %bitcast.385), kind=kOutput, calls=%fused_computation.3 | convolution fusion | flops 709628416 | bytes 45031424 | tf_op jit(solution)/shard_map/lhe,khe->hlk/dot_general | solution.py:84
  209.8 15.1 %multiply_convert_fusion.1 = bf16[8,448,1500]{2,1,0:T(8,128)(2,1)S(1)} fusion(f32[8,448,1500]{2,1,0:T(8,128)} %get-tuple-element.245, f32[8,448,1500]{2,1,0:T(8,128)} %copy-done.1, f32[8,448]{1,0:T(8,128)S(1)} %get-tuple-element.244, f32[8,448]{1,0:T(8,128)S(1)} %log_add_fusion.2), kind=kLoop, calls=%fused_computation.2 | loop fusion | flops 26880000 | bytes 53788672 | tf_op jit(solution)/shard_map/convert_element_type | solution.py:86
  224.9 4.8 convert_reduce_fusion.9
  241.9 5.5 fusion.222
  247.5 5.9 collective-permute-done.7
  265.2 9.0 multiply_reduce_fusion.5
  274.9 5.5 multiply_convert_fusion.3
  291.5 5.0 fusion.35
  299.2 5.5 collective-permute-done.3
  314.7 5.7 exponential_reduce_fusion
  322.5 10.1 fusion.138
  335.8 10.9 convert_reduce_fusion.3
  346.8 6.4 collective-permute-done.4
  358.9 4.0 convert_reduce_fusion
  372.5 15.9 %collective-permute-done.9 = bf16[448,1024]{1,0:T(8,128)(2,1)S(1)} collective-permute-done((bf16[448,1024]{1,0:T(8,128)(2,1)S(1)}, bf16[448,1024]{1,0:T(8,128)(2,1)S(1)}, u32[]{:S(2)}, u32[]{:S(2)}) %collective-permute-start.9) | collective-permute-done | bytes 917536 | tf_op jit(solution)/shard_map/ppermute | solution.py:121
  389.9 12.5 collective-permute-done.5
  415.2 12.0 convert_reduce_fusion.2
  428.3 5.5 fusion.113
  433.8 15.4 %multiply_reduce_fusion = (f32[8,448]{1,0:T(8,128)S(1)}, f32[8,448,1500]{2,1,0:T(8,128)}) fusion(f32[8,448,1500]{2,1,0:T(8,128)} %copy-done.2, f32[8,448]{1,0:T(8,128)S(1)} %log_add_fusion, bf16[448,8,64]{0,2,1:T(8,128)(2,1)} %bitcast.399, bf16[1500,8,64]{0,2,1:T(8,128)(2,1)} %bitcast.382), kind=kOutput, calls=%fused_computation.1 | convolution fusion | flops 709628416 | bytes 45031424 | tf_op jit(solution)/shard_map/lhe,khe->hlk/dot_general | solution.py:84
  449.4 14.9 %multiply_convert_fusion = bf16[8,448,1500]{2,1,0:T(8,128)(2,1)S(1)} fusion(f32[8,448,1500]{2,1,0:T(8,128)} %get-tuple-element.252, f32[8,448,1500]{2,1,0:T(8,128)} %copy-done.2, f32[8,448]{1,0:T(8,128)S(1)} %get-tuple-element.251, f32[8,448]{1,0:T(8,128)S(1)} %log_add_fusion), kind=kLoop, calls=%fused_computation | loop fusion | flops 26880000 | bytes 53788672 | tf_op jit(solution)/shard_map/convert_element_type | solution.py:86
  472.2 5.4 fusion.110
  477.6 8.1 convert_reduce_fusion.8
  495.5 8.9 collective-permute-done.10
  514.8 5.9 convert_reduce_fusion.11
  521.6 5.2 convert_reduce_fusion.10
  530.7 4.7 multiply_reduce_fusion.4
  535.4 4.2 multiply_convert_fusion.2
  552.5 8.9 convolution_convert_fusion.1
  573.8 28.4 %collective-permute-done.12 = bf16[1500,512]{1,0:T(8,128)(2,1)S(1)} collective-permute-done((bf16[1500,512]{1,0:T(8,128)(2,1)S(1)}, bf16[1500,512]{1,0:T(8,128)(2,1)S(1)}, u32[]{:S(2)}, u32[]{:S(2)}) %collective-permute-start.12) | collective-permute-done | bytes 1536032 | tf_op jit(solution)/shard_map/ppermute | solution.py:323
  605.0 6.2 convolution_convert_fusion
  616.6 4.8 fusion.37
  634.9 22.7 %collective-permute-done.13 = bf16[1500,512]{1,0:T(8,128)(2,1)} collective-permute-done((bf16[1500,512]{1,0:T(8,128)(2,1)}, bf16[1500,512]{1,0:T(8,128)(2,1)}, u32[]{:S(2)}, u32[]{:S(2)}) %collective-permute-start.13) | collective-permute-done | bytes 1536032 | tf_op jit(solution)/shard_map/ppermute | solution.py:323
  657.6 4.2 add_bitcast_fusion
  665.3 12.9 copy.122
  701.0 4.1 fusion.70
  718.5 61.2 %psum.7 = f32[13312]{0:T(1024)} all-reduce(f32[13312]{0:T(1024)} %add_dynamic-update-slice_fusion), channel_id=1, replica_groups=mesh['dp'=16,'tensor'=2] {'dp'}, use_global_device_ids=true, to_apply=%region_64.65 | all-reduce | flops 13312 | bytes 106496 | tf_op jit(solution)/shard_map/psum | solution.py:356
  781.1 4.1 fusion.69
  803.1 96.1 %reduce-scatter.11.cloned.1.call-done = bf16[64,512]{1,0:T(8,128)(2,1)} async-done(((bf16[1024,512]{1,0:T(8,128)(2,1)}), bf16[64,512]{1,0:T(8,128)(2,1)}) %reduce-scatter.11.cloned.1.call-update) | async-done | bytes 65552 | tf_op jit(solution)/shard_map/reduce_scatter | solution.py:126
  900.2 59.4 %reduce-scatter.13.cloned.1.call-done = bf16[64,512]{1,0:T(8,128)(2,1)} async-done(((bf16[1024,512]{1,0:T(8,128)(2,1)}), bf16[64,512]{1,0:T(8,128)(2,1)}) %reduce-scatter.13.cloned.1.call-update) | async-done | bytes 65552 | tf_op jit(solution)/shard_map/reduce_scatter | solution.py:126
  982.4 14.4 %collective-permute-done.24 = bf16[4,64,512]{2,1,0:T(8,128)(2,1)S(1)} collective-permute-done((bf16[4,64,512]{2,1,0:T(8,128)(2,1)S(1)}, bf16[4,64,512]{2,1,0:T(8,128)(2,1)S(1)}, u32[]{:S(2)}, u32[]{:S(2)}) %collective-permute-start.24) | collective-permute-done | bytes 262176 | tf_op jit(solution)/shard_map/ppermute | solution.py:25
  1000.8 19.1 %collective-permute-done.16 = bf16[4,64,512]{2,1,0:T(8,128)(2,1)S(1)} collective-permute-done((bf16[4,64,512]{2,1,0:T(8,128)(2,1)S(1)}, bf16[4,64,512]{2,1,0:T(8,128)(2,1)S(1)}, u32[]{:S(2)}, u32[]{:S(2)}) %collective-permute-start.16) | collective-permute-done | bytes 262176 | tf_op jit(solution)/shard_map/ppermute | solution.py:25
  1021.5 6.9 collective-permute-done.20
  1030.9 59.8 %reduce-scatter.27.cloned.1.call-done = bf16[64,2048]{1,0:T(8,128)(2,1)} async-done(((bf16[1024,2048]{1,0:T(8,128)(2,1)}), bf16[64,2048]{1,0:T(8,128)(2,1)}) %reduce-scatter.27.cloned.1.call-update) | async-done | bytes 262160 | tf_op jit(solution)/shard_map/reduce_scatter | solution.py:126
  1095.7 89.1 %reduce-scatter.29.cloned.1.call-done = bf16[128,1024]{1,0:T(8,128)(2,1)} async-done(((bf16[2048,1024]{1,0:T(8,128)(2,1)}), bf16[128,1024]{1,0:T(8,128)(2,1)}) %reduce-scatter.29.cloned.1.call-update) | async-done | bytes 262160 | tf_op jit(solution)/shard_map/reduce_scatter | solution.py:126
  1191.2 10.1 collective-permute-done.51
  1201.3 10.4 collective-permute-done.48
  1220.0 60.6 %collective-permute-done.52 = bf16[4,128,1024]{2,1,0:T(8,128)(2,1)S(1)} collective-permute-done((bf16[4,128,1024]{2,1,0:T(8,128)(2,1)S(1)}, bf16[4,128,1024]{2,1,0:T(8,128)(2,1)S(1)}, u32[]{:S(2)}, u32[]{:S(2)}) %collective-permute-start.52) | collective-permute-done | bytes 1048608 | tf_op jit(solution)/shard_map/ppermute | solution.py:25
  1285.7 64.7 %collective-permute-done.49 = bf16[8,64,2048]{2,1,0:T(8,128)(2,1)S(1)} collective-permute-done((bf16[8,64,2048]{2,1,0:T(8,128)(2,1)S(1)}, bf16[8,64,2048]{2,1,0:T(8,128)(2,1)S(1)}, u32[]{:S(2)}, u32[]{:S(2)}) %collective-permute-start.49) | collective-permute-done | bytes 2097184 | tf_op jit(solution)/shard_map/ppermute | solution.py:25
  1351.1 4.7 bitcast_convert_fusion.1
  1355.8 39.2 %collective-permute-done.53 = bf16[8,128,1024]{2,1,0:T(8,128)(2,1)S(1)} collective-permute-done((bf16[8,128,1024]{2,1,0:T(8,128)(2,1)S(1)}, bf16[8,128,1024]{2,1,0:T(8,128)(2,1)S(1)}, u32[]{:S(2)}, u32[]{:S(2)}) %collective-permute-start.53) | collective-permute-done | bytes 2097184 | tf_op jit(solution)/shard_map/ppermute | solution.py:25
  1395.7 4.7 bitcast_convert_fusion
  (765 shorter events, 353.7 us)
Async XLA Ops:
  7.2 654.5 %reduce-scatter.25.cloned.1.call-start = ((), (), s32[]{:S(2)}) async-start(), calls=%async_computation.17 | async-start | bytes 1114112 | tf_op jit(solution)/shard_map/reduce_scatter | solution.py:126
  38.4 35.6 %collective-permute-start = (bf16[448,1024]{1,0:T(8,128)(2,1)}, bf16[448,1024]{1,0:T(8,128)(2,1)}, u32[]{:S(2)}, u32[]{:S(2)}) collective-permute-start(bf16[448,1024]{1,0:T(8,128)(2,1)} %convolution_convert_fusion.14), channel_id=1, source_target_pairs={{0,1},{1,0},{2,3},{3,2},{4,5},{5,4},{6,7},{7,6},{8,9},{9,8},{10,11... | collective-permute-start | bytes 2752520 | tf_op jit(solution)/shard_map/ppermute | solution.py:121
  108.2 21.9 %collective-permute-start.1 = (bf16[448,1024]{1,0:T(8,128)(2,1)S(1)}, bf16[448,1024]{1,0:T(8,128)(2,1)S(1)}, u32[]{:S(2)}, u32[]{:S(2)}) collective-permute-start(bf16[448,1024]{1,0:T(8,128)(2,1)S(1)} %convolution_convert_fusion.13), channel_id=1, source_target_pairs={{0,1},{1,0},{2,3},{3,2},{4,5},{5,4},{6,7},{7,6},{8,9},{9,8},{10,11... | collective-permute-start | bytes 2752520 | tf_op jit(solution)/shard_map/ppermute | solution.py:121
  143.5 23.5 %collective-permute-start.6 = (bf16[448,1024]{1,0:T(8,128)(2,1)}, bf16[448,1024]{1,0:T(8,128)(2,1)}, u32[]{:S(2)}, u32[]{:S(2)}) collective-permute-start(bf16[448,1024]{1,0:T(8,128)(2,1)} %convolution_convert_fusion.16), channel_id=1, source_target_pairs={{0,1},{1,0},{2,3},{3,2},{4,5},{5,4},{6,7},{7,6},{8,9},{9,8},{10,11... | collective-permute-start | bytes 2752520 | tf_op jit(solution)/shard_map/ppermute | solution.py:121
  146.8 37.7 %collective-permute-start.2 = (bf16[448,1024]{1,0:T(8,128)(2,1)}, bf16[448,1024]{1,0:T(8,128)(2,1)}, u32[]{:S(2)}, u32[]{:S(2)}) collective-permute-start(bf16[448,1024]{1,0:T(8,128)(2,1)} %convolution_convert_fusion.18), channel_id=1, source_target_pairs={{0,1},{1,0},{2,3},{3,2},{4,5},{5,4},{6,7},{7,6},{8,9},{9,8},{10,11... | collective-permute-start | bytes 2752520 | tf_op jit(solution)/shard_map/ppermute | solution.py:121
  233.0 20.4 %collective-permute-start.7 = (bf16[448,1024]{1,0:T(8,128)(2,1)}, bf16[448,1024]{1,0:T(8,128)(2,1)}, u32[]{:S(2)}, u32[]{:S(2)}) collective-permute-start(bf16[448,1024]{1,0:T(8,128)(2,1)} %convolution_convert_fusion.10), channel_id=1, source_target_pairs={{0,1},{1,0},{2,3},{3,2},{4,5},{5,4},{6,7},{7,6},{8,9},{9,8},{10,11... | collective-permute-start | bytes 2752520 | tf_op jit(solution)/shard_map/ppermute | solution.py:121
  285.2 19.6 %collective-permute-start.3 = (bf16[448,1024]{1,0:T(8,128)(2,1)}, bf16[448,1024]{1,0:T(8,128)(2,1)}, u32[]{:S(2)}, u32[]{:S(2)}) collective-permute-start(bf16[448,1024]{1,0:T(8,128)(2,1)} %convolution_convert_fusion.12), channel_id=1, source_target_pairs={{0,1},{1,0},{2,3},{3,2},{4,5},{5,4},{6,7},{7,6},{8,9},{9,8},{10,11... | collective-permute-start | bytes 2752520 | tf_op jit(solution)/shard_map/ppermute | solution.py:121
  334.7 18.5 %collective-permute-start.4 = (bf16[448,1024]{1,0:T(8,128)(2,1)S(1)}, bf16[448,1024]{1,0:T(8,128)(2,1)S(1)}, u32[]{:S(2)}, u32[]{:S(2)}) collective-permute-start(bf16[448,1024]{1,0:T(8,128)(2,1)S(1)} %convolution_convert_fusion.11), channel_id=1, source_target_pairs={{0,1},{1,0},{2,3},{3,2},{4,5},{5,4},{6,7},{7,6},{8,9},{9,8},{10,11... | collective-permute-start | bytes 2752520 | tf_op jit(solution)/shard_map/ppermute | solution.py:121
  365.1 23.3 %collective-permute-start.9 = (bf16[448,1024]{1,0:T(8,128)(2,1)S(1)}, bf16[448,1024]{1,0:T(8,128)(2,1)S(1)}, u32[]{:S(2)}, u32[]{:S(2)}) collective-permute-start(bf16[448,1024]{1,0:T(8,128)(2,1)S(1)} %convolution_convert_fusion.15), channel_id=1, source_target_pairs={{0,1},{1,0},{2,3},{3,2},{4,5},{5,4},{6,7},{7,6},{8,9},{9,8},{10,11... | collective-permute-start | bytes 2752520 | tf_op jit(solution)/shard_map/ppermute | solution.py:121
  368.6 33.8 %collective-permute-start.5 = (bf16[448,1024]{1,0:T(8,128)(2,1)S(1)}, bf16[448,1024]{1,0:T(8,128)(2,1)S(1)}, u32[]{:S(2)}, u32[]{:S(2)}) collective-permute-start(bf16[448,1024]{1,0:T(8,128)(2,1)S(1)} %convolution_convert_fusion.17), channel_id=1, source_target_pairs={{0,1},{1,0},{2,3},{3,2},{4,5},{5,4},{6,7},{7,6},{8,9},{9,8},{10,11... | collective-permute-start | bytes 2752520 | tf_op jit(solution)/shard_map/ppermute | solution.py:121
  412.7 265.5 %reduce-scatter.23.cloned.1.call-start = ((), (), s32[]{:S(2)}) async-start(), calls=%async_computation.16 | async-start | bytes 1114112 | tf_op jit(solution)/shard_map/reduce_scatter | solution.py:126
  449.2 229.6 %reduce-scatter.21.cloned.1.call-start = ((), (), s32[]{:S(2)}) async-start(), calls=%async_computation.15 | async-start | bytes 1114112 | tf_op jit(solution)/shard_map/reduce_scatter | solution.py:126
  477.6 201.3 %reduce-scatter.19.cloned.1.call-start = ((), (), s32[]{:S(2)}) async-start(), calls=%async_computation.14 | async-start | bytes 1114112 | tf_op jit(solution)/shard_map/reduce_scatter | solution.py:126
  487.5 16.9 %collective-permute-start.10 = (bf16[448,1024]{1,0:T(8,128)(2,1)}, bf16[448,1024]{1,0:T(8,128)(2,1)}, u32[]{:S(2)}, u32[]{:S(2)}) collective-permute-start(bf16[448,1024]{1,0:T(8,128)(2,1)} %convolution_convert_fusion.9), channel_id=1, source_target_pairs={{0,1},{1,0},{2,3},{3,2},{4,5},{5,4},{6,7},{7,6},{8,9},{9,8},{10,11... | collective-permute-start | bytes 2752520 | tf_op jit(solution)/shard_map/ppermute | solution.py:121
  491.6 306.6 %reduce-scatter.17.cloned.1.call-start = ((), (), s32[]{:S(2)}) async-start(), calls=%async_computation.13 | async-start | bytes 1114112 | tf_op jit(solution)/shard_map/reduce_scatter | solution.py:126
  514.7 287.4 %reduce-scatter.15.cloned.1.call-start = ((), (), s32[]{:S(2)}) async-start(), calls=%async_computation.12 | async-start | bytes 1114112 | tf_op jit(solution)/shard_map/reduce_scatter | solution.py:126
  530.2 369.1 %reduce-scatter.11.cloned.1.call-start = ((), (), s32[]{:S(2)}) async-start(), calls=%async_computation.10 | async-start | bytes 1114112 | tf_op jit(solution)/shard_map/reduce_scatter | solution.py:126
  544.8 414.8 %reduce-scatter.13.cloned.1.call-start = ((), (), s32[]{:S(2)}) async-start(), calls=%async_computation.11 | async-start | bytes 1114112 | tf_op jit(solution)/shard_map/reduce_scatter | solution.py:126
  552.5 538.2 %reduce-scatter.27.cloned.1.call-start = ((), (), s32[]{:S(2)}) async-start(), calls=%async_computation.18 | async-start | bytes 4456448 | tf_op jit(solution)/shard_map/reduce_scatter | solution.py:126
  561.5 623.2 %reduce-scatter.29.cloned.1.call-start = ((), (), s32[]{:S(2)}) async-start(), calls=%async_computation.19 | async-start | bytes 4456448 | tf_op jit(solution)/shard_map/reduce_scatter | solution.py:126
  565.6 36.6 %collective-permute-start.12 = (bf16[1500,512]{1,0:T(8,128)(2,1)S(1)}, bf16[1500,512]{1,0:T(8,128)(2,1)S(1)}, u32[]{:S(2)}, u32[]{:S(2)}) collective-permute-start(bf16[1500,512]{1,0:T(8,128)(2,1)S(1)} %fusion.36), channel_id=1, source_target_pairs={{0,1},{1,0},{2,3},{3,2},{4,5},{5,4},{6,7},{7,6},{8,9},{9,8},{10,11... | collective-permute-start | bytes 4608008 | tf_op jit(solution)/shard_map/ppermute | solution.py:323
  573.4 126.3 %collective-permute-start.8 = (bf16[448,1024]{1,0:T(8,128)(2,1)}, bf16[448,1024]{1,0:T(8,128)(2,1)}, u32[]{:S(2)}, u32[]{:S(2)}) collective-permute-start(bf16[448,1024]{1,0:T(8,128)(2,1)} %add_convert_fusion.1), channel_id=1, source_target_pairs={{0,1},{1,0},{2,3},{3,2},{4,5},{5,4},{6,7},{7,6},{8,9},{9,8},{10,11... | collective-permute-start | bytes 2752520 | tf_op jit(solution)/shard_map/ppermute | solution.py:121
  621.4 36.2 %collective-permute-start.13 = (bf16[1500,512]{1,0:T(8,128)(2,1)}, bf16[1500,512]{1,0:T(8,128)(2,1)}, u32[]{:S(2)}, u32[]{:S(2)}) collective-permute-start(bf16[1500,512]{1,0:T(8,128)(2,1)} %fusion.37), channel_id=1, source_target_pairs={{0,1},{1,0},{2,3},{3,2},{4,5},{5,4},{6,7},{7,6},{8,9},{9,8},{10,11... | collective-permute-start | bytes 4608008 | tf_op jit(solution)/shard_map/ppermute | solution.py:323
  634.6 66.3 %collective-permute-start.11 = (bf16[448,1024]{1,0:T(8,128)(2,1)}, bf16[448,1024]{1,0:T(8,128)(2,1)}, u32[]{:S(2)}, u32[]{:S(2)}) collective-permute-start(bf16[448,1024]{1,0:T(8,128)(2,1)} %add_convert_fusion), channel_id=1, source_target_pairs={{0,1},{1,0},{2,3},{3,2},{4,5},{5,4},{6,7},{7,6},{8,9},{9,8},{10,11... | collective-permute-start | bytes 2752520 | tf_op jit(solution)/shard_map/ppermute | solution.py:121
  661.7 17.2 %collective-permute-start.42 = (bf16[1,32,1024]{2,1,0:T(8,128)(2,1)}, bf16[1,32,1024]{2,1,0:T(8,128)(2,1)S(1)}, u32[]{:S(2)}, u32[]{:S(2)}) collective-permute-start(bf16[1,32,1024]{2,1,0:T(8,128)(2,1)} %bitcast.442), channel_id=1, source_target_pairs={{0,2},{2,0},{4,6},{6,4},{8,10},{10,8},{12,14},{14,12},{16,18},{18,... | collective-permute-start | bytes 196616 | tf_op jit(solution)/shard_map/ppermute | solution.py:25
  678.2 1.7 collective-permute-start.38
  678.8 3.2 collective-permute-start.34
  678.9 4.9 collective-permute-start.30
  679.9 8.9 collective-permute-start.43
  682.0 9.6 collective-permute-start.39
  683.8 10.6 collective-permute-start.35
  688.8 8.4 collective-permute-start.31
  691.6 97.1 %collective-permute-start.44 = (bf16[4,32,1024]{2,1,0:T(8,128)(2,1)}, bf16[4,32,1024]{2,1,0:T(8,128)(2,1)}, u32[]{:S(2)}, u32[]{:S(2)}) collective-permute-start(bf16[4,32,1024]{2,1,0:T(8,128)(2,1)} %pad_maximum_fusion.45), channel_id=1, source_target_pairs={{0,8},{2,10},{4,12},{6,14},{8,0},{10,2},{12,4},{14,6},{16,24},{18,... | collective-permute-start | bytes 786440 | tf_op jit(solution)/shard_map/ppermute | solution.py:25
  694.4 96.2 %collective-permute-start.40 = (bf16[4,64,512]{2,1,0:T(8,128)(2,1)}, bf16[4,64,512]{2,1,0:T(8,128)(2,1)}, u32[]{:S(2)}, u32[]{:S(2)}) collective-permute-start(bf16[4,64,512]{2,1,0:T(8,128)(2,1)} %pad_maximum_fusion.44), channel_id=1, source_target_pairs={{0,8},{2,10},{4,12},{6,14},{8,0},{10,2},{12,4},{14,6},{16,24},{18,... | collective-permute-start | bytes 786440 | tf_op jit(solution)/shard_map/ppermute | solution.py:25
  697.2 98.1 %collective-permute-start.36 = (bf16[4,64,512]{2,1,0:T(8,128)(2,1)}, bf16[4,64,512]{2,1,0:T(8,128)(2,1)}, u32[]{:S(2)}, u32[]{:S(2)}) collective-permute-start(bf16[4,64,512]{2,1,0:T(8,128)(2,1)} %pad_maximum_fusion.43), channel_id=1, source_target_pairs={{0,8},{2,10},{4,12},{6,14},{8,0},{10,2},{12,4},{14,6},{16,24},{18,... | collective-permute-start | bytes 786440 | tf_op jit(solution)/shard_map/ppermute | solution.py:25
  699.8 97.5 %collective-permute-start.32 = (bf16[4,64,512]{2,1,0:T(8,128)(2,1)}, bf16[4,64,512]{2,1,0:T(8,128)(2,1)}, u32[]{:S(2)}, u32[]{:S(2)}) collective-permute-start(bf16[4,64,512]{2,1,0:T(8,128)(2,1)} %pad_maximum_fusion.42), channel_id=1, source_target_pairs={{0,8},{2,10},{4,12},{6,14},{8,0},{10,2},{12,4},{14,6},{16,24},{18,... | collective-permute-start | bytes 786440 | tf_op jit(solution)/shard_map/ppermute | solution.py:25
  790.6 172.7 %collective-permute-start.45 = (bf16[8,32,1024]{2,1,0:T(8,128)(2,1)}, bf16[8,32,1024]{2,1,0:T(8,128)(2,1)}, u32[]{:S(2)}, u32[]{:S(2)}) collective-permute-start(bf16[8,32,1024]{2,1,0:T(8,128)(2,1)} %pad_maximum_fusion.35), channel_id=1, source_target_pairs={{0,16},{2,18},{4,20},{6,22},{8,24},{10,26},{12,28},{14,30},{16,0},... | collective-permute-start | bytes 1572872 | tf_op jit(solution)/shard_map/ppermute | solution.py:25
  792.5 172.8 %collective-permute-start.41 = (bf16[8,64,512]{2,1,0:T(8,128)(2,1)}, bf16[8,64,512]{2,1,0:T(8,128)(2,1)}, u32[]{:S(2)}, u32[]{:S(2)}) collective-permute-start(bf16[8,64,512]{2,1,0:T(8,128)(2,1)} %pad_maximum_fusion.34), channel_id=1, source_target_pairs={{0,16},{2,18},{4,20},{6,22},{8,24},{10,26},{12,28},{14,30},{16,0},... | collective-permute-start | bytes 1572872 | tf_op jit(solution)/shard_map/ppermute | solution.py:25
  797.2 170.6 %collective-permute-start.37 = (bf16[8,64,512]{2,1,0:T(8,128)(2,1)}, bf16[8,64,512]{2,1,0:T(8,128)(2,1)}, u32[]{:S(2)}, u32[]{:S(2)}) collective-permute-start(bf16[8,64,512]{2,1,0:T(8,128)(2,1)} %pad_maximum_fusion.33), channel_id=1, source_target_pairs={{0,16},{2,18},{4,20},{6,22},{8,24},{10,26},{12,28},{14,30},{16,0},... | collective-permute-start | bytes 1572872 | tf_op jit(solution)/shard_map/ppermute | solution.py:25
  798.3 3.8 collective-permute-start.26
  799.2 170.7 %collective-permute-start.33 = (bf16[8,64,512]{2,1,0:T(8,128)(2,1)}, bf16[8,64,512]{2,1,0:T(8,128)(2,1)}, u32[]{:S(2)}, u32[]{:S(2)}) collective-permute-start(bf16[8,64,512]{2,1,0:T(8,128)(2,1)} %pad_maximum_fusion.32), channel_id=1, source_target_pairs={{0,16},{2,18},{4,20},{6,22},{8,24},{10,26},{12,28},{14,30},{16,0},... | collective-permute-start | bytes 1572872 | tf_op jit(solution)/shard_map/ppermute | solution.py:25
  802.1 97.2 %collective-permute-start.22 = (bf16[1,64,512]{2,1,0:T(8,128)(2,1)}, bf16[1,64,512]{2,1,0:T(8,128)(2,1)S(1)}, u32[]{:S(2)}, u32[]{:S(2)}) collective-permute-start(bf16[1,64,512]{2,1,0:T(8,128)(2,1)} %bitcast.439), channel_id=1, source_target_pairs={{0,2},{2,0},{4,6},{6,4},{8,10},{10,8},{12,14},{14,12},{16,18},{18,... | collective-permute-start | bytes 196616 | tf_op jit(solution)/shard_map/ppermute | solution.py:25
  899.3 60.3 %collective-permute-start.14 = (bf16[1,64,512]{2,1,0:T(8,128)(2,1)}, bf16[1,64,512]{2,1,0:T(8,128)(2,1)}, u32[]{:S(2)}, u32[]{:S(2)}) collective-permute-start(bf16[1,64,512]{2,1,0:T(8,128)(2,1)} %bitcast.440), channel_id=1, source_target_pairs={{0,2},{2,0},{4,6},{6,4},{8,10},{10,8},{12,14},{14,12},{16,18},{18,... | collective-permute-start | bytes 196616 | tf_op jit(solution)/shard_map/ppermute | solution.py:25
  959.6 1.5 collective-permute-start.18
  961.1 16.8 %collective-permute-start.27 = (bf16[2,32,1024]{2,1,0:T(8,128)(2,1)S(1)}, bf16[2,32,1024]{2,1,0:T(8,128)(2,1)S(1)}, u32[]{:S(2)}, u32[]{:S(2)}) collective-permute-start(bf16[2,32,1024]{2,1,0:T(8,128)(2,1)S(1)} %pad_maximum_fusion.49), channel_id=1, source_target_pairs={{0,4},{2,6},{4,0},{6,2},{8,12},{10,14},{12,8},{14,10},{16,20},{18,... | collective-permute-start | bytes 393224 | tf_op jit(solution)/shard_map/ppermute | solution.py:25
  963.3 16.0 %collective-permute-start.23 = (bf16[2,64,512]{2,1,0:T(8,128)(2,1)S(1)}, bf16[2,64,512]{2,1,0:T(8,128)(2,1)S(1)}, u32[]{:S(2)}, u32[]{:S(2)}) collective-permute-start(bf16[2,64,512]{2,1,0:T(8,128)(2,1)S(1)} %pad_maximum_fusion.48), channel_id=1, source_target_pairs={{0,4},{2,6},{4,0},{6,2},{8,12},{10,14},{12,8},{14,10},{16,20},{18,... | collective-permute-start | bytes 393224 | tf_op jit(solution)/shard_map/ppermute | solution.py:25
  965.3 14.8 %collective-permute-start.15 = (bf16[2,64,512]{2,1,0:T(8,128)(2,1)S(1)}, bf16[2,64,512]{2,1,0:T(8,128)(2,1)S(1)}, u32[]{:S(2)}, u32[]{:S(2)}) collective-permute-start(bf16[2,64,512]{2,1,0:T(8,128)(2,1)S(1)} %pad_maximum_fusion.46), channel_id=1, source_target_pairs={{0,4},{2,6},{4,0},{6,2},{8,12},{10,14},{12,8},{14,10},{16,20},{18,... | collective-permute-start | bytes 393224 | tf_op jit(solution)/shard_map/ppermute | solution.py:25
  967.8 13.8 collective-permute-start.19
  977.9 19.1 %collective-permute-start.28 = (bf16[4,32,1024]{2,1,0:T(8,128)(2,1)S(1)}, bf16[4,32,1024]{2,1,0:T(8,128)(2,1)S(1)}, u32[]{:S(2)}, u32[]{:S(2)}) collective-permute-start(bf16[4,32,1024]{2,1,0:T(8,128)(2,1)S(1)} %pad_maximum_fusion.41), channel_id=1, source_target_pairs={{0,8},{2,10},{4,12},{6,14},{8,0},{10,2},{12,4},{14,6},{16,24},{18,... | collective-permute-start | bytes 786440 | tf_op jit(solution)/shard_map/ppermute | solution.py:25
  979.4 17.5 %collective-permute-start.24 = (bf16[4,64,512]{2,1,0:T(8,128)(2,1)S(1)}, bf16[4,64,512]{2,1,0:T(8,128)(2,1)S(1)}, u32[]{:S(2)}, u32[]{:S(2)}) collective-permute-start(bf16[4,64,512]{2,1,0:T(8,128)(2,1)S(1)} %pad_maximum_fusion.40), channel_id=1, source_target_pairs={{0,8},{2,10},{4,12},{6,14},{8,0},{10,2},{12,4},{14,6},{16,24},{18,... | collective-permute-start | bytes 786440 | tf_op jit(solution)/shard_map/ppermute | solution.py:25
  980.2 39.7 %collective-permute-start.16 = (bf16[4,64,512]{2,1,0:T(8,128)(2,1)S(1)}, bf16[4,64,512]{2,1,0:T(8,128)(2,1)S(1)}, u32[]{:S(2)}, u32[]{:S(2)}) collective-permute-start(bf16[4,64,512]{2,1,0:T(8,128)(2,1)S(1)} %pad_maximum_fusion.38), channel_id=1, source_target_pairs={{0,8},{2,10},{4,12},{6,14},{8,0},{10,2},{12,4},{14,6},{16,24},{18,... | collective-permute-start | bytes 786440 | tf_op jit(solution)/shard_map/ppermute | solution.py:25
  981.6 46.8 %collective-permute-start.20 = (bf16[4,64,512]{2,1,0:T(8,128)(2,1)S(1)}, bf16[4,64,512]{2,1,0:T(8,128)(2,1)S(1)}, u32[]{:S(2)}, u32[]{:S(2)}) collective-permute-start(bf16[4,64,512]{2,1,0:T(8,128)(2,1)S(1)} %pad_maximum_fusion.39), channel_id=1, source_target_pairs={{0,8},{2,10},{4,12},{6,14},{8,0},{10,2},{12,4},{14,6},{16,24},{18,... | collective-permute-start | bytes 786440 | tf_op jit(solution)/shard_map/ppermute | solution.py:25
  996.9 93.8 %collective-permute-start.25 = (bf16[8,64,512]{2,1,0:T(8,128)(2,1)S(1)}, bf16[8,64,512]{2,1,0:T(8,128)(2,1)S(1)}, u32[]{:S(2)}, u32[]{:S(2)}) collective-permute-start(bf16[8,64,512]{2,1,0:T(8,128)(2,1)S(1)} %pad_maximum_fusion.30), channel_id=1, source_target_pairs={{0,16},{2,18},{4,20},{6,22},{8,24},{10,26},{12,28},{14,30},{16,0},... | collective-permute-start | bytes 1572872 | tf_op jit(solution)/shard_map/ppermute | solution.py:25
  997.9 96.5 %collective-permute-start.29 = (bf16[8,32,1024]{2,1,0:T(8,128)(2,1)}, bf16[8,32,1024]{2,1,0:T(8,128)(2,1)}, u32[]{:S(2)}, u32[]{:S(2)}) collective-permute-start(bf16[8,32,1024]{2,1,0:T(8,128)(2,1)} %pad_maximum_fusion.31), channel_id=1, source_target_pairs={{0,16},{2,18},{4,20},{6,22},{8,24},{10,26},{12,28},{14,30},{16,0},... | collective-permute-start | bytes 1572872 | tf_op jit(solution)/shard_map/ppermute | solution.py:25
  1021.5 167.4 %collective-permute-start.17 = (bf16[8,64,512]{2,1,0:T(8,128)(2,1)}, bf16[8,64,512]{2,1,0:T(8,128)(2,1)}, u32[]{:S(2)}, u32[]{:S(2)}) collective-permute-start(bf16[8,64,512]{2,1,0:T(8,128)(2,1)} %pad_maximum_fusion.28), channel_id=1, source_target_pairs={{0,16},{2,18},{4,20},{6,22},{8,24},{10,26},{12,28},{14,30},{16,0},... | collective-permute-start | bytes 1572872 | tf_op jit(solution)/shard_map/ppermute | solution.py:25
  1030.0 160.0 %collective-permute-start.21 = (bf16[8,64,512]{2,1,0:T(8,128)(2,1)}, bf16[8,64,512]{2,1,0:T(8,128)(2,1)}, u32[]{:S(2)}, u32[]{:S(2)}) collective-permute-start(bf16[8,64,512]{2,1,0:T(8,128)(2,1)} %pad_maximum_fusion.29), channel_id=1, source_target_pairs={{0,16},{2,18},{4,20},{6,22},{8,24},{10,26},{12,28},{14,30},{16,0},... | collective-permute-start | bytes 1572872 | tf_op jit(solution)/shard_map/ppermute | solution.py:25
  1090.7 1.7 collective-permute-start.46
  1093.4 91.3 %collective-permute-start.47 = (bf16[2,64,2048]{2,1,0:T(8,128)(2,1)}, bf16[2,64,2048]{2,1,0:T(8,128)(2,1)}, u32[]{:S(2)}, u32[]{:S(2)}) collective-permute-start(bf16[2,64,2048]{2,1,0:T(8,128)(2,1)} %pad_maximum_fusion.36), channel_id=1, source_target_pairs={{0,4},{2,6},{4,0},{6,2},{8,12},{10,14},{12,8},{14,10},{16,20},{18,... | collective-permute-start | bytes 1572872 | tf_op jit(solution)/shard_map/ppermute | solution.py:25
  1184.7 2.3 collective-permute-start.50
  1186.2 25.6 %collective-permute-start.48 = (bf16[4,64,2048]{2,1,0:T(8,128)(2,1)S(1)}, bf16[4,64,2048]{2,1,0:T(8,128)(2,1)S(1)}, u32[]{:S(2)}, u32[]{:S(2)}) collective-permute-start(bf16[4,64,2048]{2,1,0:T(8,128)(2,1)S(1)} %pad_maximum_fusion.23), channel_id=1, source_target_pairs={{0,8},{2,10},{4,12},{6,14},{8,0},{10,2},{12,4},{14,6},{16,24},{18,... | collective-permute-start | bytes 3145736 | tf_op jit(solution)/shard_map/ppermute | solution.py:25
  1187.2 14.1 %collective-permute-start.51 = (bf16[2,128,1024]{2,1,0:T(8,128)(2,1)S(1)}, bf16[2,128,1024]{2,1,0:T(8,128)(2,1)S(1)}, u32[]{:S(2)}, u32[]{:S(2)}) collective-permute-start(bf16[2,128,1024]{2,1,0:T(8,128)(2,1)S(1)} %pad_maximum_fusion.37), channel_id=1, source_target_pairs={{0,4},{2,6},{4,0},{6,2},{8,12},{10,14},{12,8},{14,10},{16,20},{18,... | collective-permute-start | bytes 1572872 | tf_op jit(solution)/shard_map/ppermute | solution.py:25
  1212.1 138.3 %collective-permute-start.49 = (bf16[8,64,2048]{2,1,0:T(8,128)(2,1)S(1)}, bf16[8,64,2048]{2,1,0:T(8,128)(2,1)S(1)}, u32[]{:S(2)}, u32[]{:S(2)}) collective-permute-start(bf16[8,64,2048]{2,1,0:T(8,128)(2,1)S(1)} %pad_maximum_fusion.8), channel_id=1, source_target_pairs={{0,16},{2,18},{4,20},{6,22},{8,24},{10,26},{12,28},{14,30},{16,0},... | collective-permute-start | bytes 6291464 | tf_op jit(solution)/shard_map/ppermute | solution.py:25
  1213.6 67.1 %collective-permute-start.52 = (bf16[4,128,1024]{2,1,0:T(8,128)(2,1)S(1)}, bf16[4,128,1024]{2,1,0:T(8,128)(2,1)S(1)}, u32[]{:S(2)}, u32[]{:S(2)}) collective-permute-start(bf16[4,128,1024]{2,1,0:T(8,128)(2,1)S(1)} %pad_maximum_fusion.24), channel_id=1, source_target_pairs={{0,8},{2,10},{4,12},{6,14},{8,0},{10,2},{12,4},{14,6},{16,24},{18,... | collective-permute-start | bytes 3145736 | tf_op jit(solution)/shard_map/ppermute | solution.py:25
  1281.0 114.1 %collective-permute-start.53 = (bf16[8,128,1024]{2,1,0:T(8,128)(2,1)S(1)}, bf16[8,128,1024]{2,1,0:T(8,128)(2,1)S(1)}, u32[]{:S(2)}, u32[]{:S(2)}) collective-permute-start(bf16[8,128,1024]{2,1,0:T(8,128)(2,1)S(1)} %pad_maximum_fusion.9), channel_id=1, source_target_pairs={{0,16},{2,18},{4,20},{6,22},{8,24},{10,26},{12,28},{14,30},{16,0},... | collective-permute-start | bytes 6291464 | tf_op jit(solution)/shard_map/ppermute | solution.py:25
  (196 other events, 1766.0 us)
Sparse Core Ops, SparseCore 0:
  412.8 58.0 reduce-scatter.24
  474.5 56.6 reduce-scatter.22
  534.8 56.5 reduce-scatter.20
  594.9 56.6 reduce-scatter.18
  655.0 59.6 reduce-scatter.16
  718.2 56.6 reduce-scatter.14
  778.5 120.7 reduce-scatter.10
  902.9 56.6 reduce-scatter.12
  964.0 126.6 reduce-scatter.26
  1095.0 89.6 reduce-scatter.28
